TPU v7x, 512 devices: a whole 4x4x16 slice. The times are simulated.
512 devices in a mesh: clus: 64 (over x, z_hi, y), samp: 8 (over z_lo, core).
Axes of the slice: x: 4, y: 4, z: 16 (z_hi: 4, z_lo: 4; z = z_hi * 4 + z_lo), core: 2. Of those that a mesh axis runs over, the one named last changes fastest.
Arguments:
- child_patterns: float32 [2048, 2, 24, 512], P('clus', None, 'samp'), may hold values from -6 to 6
- theta_weights: float32 [6, 9], replicated, may hold values from -0.4 to 0.6
- phi_stencil: int32 [1024, 6], replicated, may hold values from 0 to 511, as said below
- phi_weights: float32 [1024, 6], replicated, may hold values from -0.3 to 0.7
- shift_phase: float32 [8, 48, 1024], P(None, 'samp'), may hold values from -3.140625 to 3.140625
- translation_table: float32 [16, 2, 48, 1024], P(None, None, 'samp', 'clus'), may hold values from -1.25 to 1.25
- far_list: int32 [256, 12], replicated, may hold values from 0 to 255, as said below
- far_vector: int32 [256, 12], replicated, may hold values from 0 to 15
Outputs:
- parent_incoming: float32 [256, 2, 48, 1024], P('clus', None, 'samp')
- child_incoming: float32 [2048, 2, 24, 512], P('clus', None, 'samp')
Inputs may be any that keep to these rules, and one draw needn't show every extreme that they name: `far_list`: row i names 12 different parent clusters, never i itself. `phi_stencil`: row n names 6 cyclically consecutive child columns starting at n // 2 - 6 // 2 + 1 or one column later.
All inputs are finite; a program needn't handle non-finite values.
Results may differ from a plain program's by a relative error of at most 0.00007.
Values sent between devices are 32-bit elements; how exact they have to be, the bound alone decides.
A program may use at most 128 MiB of HBM per device.

v0:
```python
import jax
import jax.numpy as jnp
from jax import lax
from jax.sharding import PartitionSpec as P

P_SIZE = 6


def padded(cells, sides, width):
    for axis, dim in sides:
        count = lax.axis_size(axis)
        head = lax.slice_in_dim(cells, 0, width, axis=dim)
        tail = lax.slice_in_dim(cells, cells.shape[dim] - width, cells.shape[dim], axis=dim)
        cells = jnp.concatenate(
            [
                lax.ppermute(tail, axis, [(i, (i + 1) % count) for i in range(count)]),
                cells,
                lax.ppermute(head, axis, [((i + 1) % count, i) for i in range(count)]),
            ],
            axis=dim,
        )
    return cells


def shifted(value, axis, by):
    peers = lax.axis_size(axis)
    return lax.ppermute(value, axis, [(i, (i + by) % peers) for i in range(peers)])


def phi_table(phi_stencil, phi_weights, columns):
    positions = jnp.arange(columns, dtype=jnp.int32)
    total = jnp.zeros((columns, phi_stencil.shape[0]), jnp.float32)
    for point in range(phi_stencil.shape[1]):
        hits = (phi_stencil[None, :, point] == positions[:, None]).astype(jnp.float32)
        total = total + hits * phi_weights[None, :, point]
    return total


def combine_pairs(patterns, table, far_ids, vec_ids):
    source = patterns[far_ids]
    operator = table[vec_ids]
    real_part = operator[:, :, 0] * source[:, :, 0] - operator[:, :, 1] * source[:, :, 1]
    imag_part = operator[:, :, 0] * source[:, :, 1] + operator[:, :, 1] * source[:, :, 0]
    return jnp.stack([jnp.sum(real_part, axis=1), jnp.sum(imag_part, axis=1)], axis=1)


def per_device(
    child_patterns,
    theta_weights,
    phi_stencil,
    phi_weights,
    shift_phase,
    translation_table,
    far_list,
    far_vector,
):
    highest = lax.Precision.HIGHEST
    groups = child_patterns.shape[0] // 8
    columns = child_patterns.shape[3]
    rows_parent = theta_weights.shape[0]
    azimuth = phi_stencil.shape[0]
    margin = P_SIZE // 2
    phi_matrix = phi_table(phi_stencil, phi_weights, columns)
    cosine = jnp.cos(shift_phase)
    sine = jnp.sin(shift_phase)
    extended = padded(child_patterns, (("samp", 2),), margin)
    spread = jnp.einsum("cqtp,pn->cqtn", extended, phi_matrix, precision=highest)
    refined = jnp.einsum("ab,cqbn->cqan", theta_weights, spread, precision=highest)
    refined = refined.reshape(groups, 8, 2, rows_parent, azimuth)
    real_part = refined[:, :, 0] * cosine - refined[:, :, 1] * sine
    imag_part = refined[:, :, 0] * sine + refined[:, :, 1] * cosine
    outgoing = jnp.stack([jnp.sum(real_part, axis=1), jnp.sum(imag_part, axis=1)], axis=1)
    everyone = lax.all_gather(outgoing, "clus", axis=0, tiled=True)
    leading = jnp.moveaxis(translation_table, 3, 0)
    gathered = lax.all_gather(leading, "clus", axis=0, tiled=True)
    table_whole = jnp.moveaxis(gathered, 0, 3)
    first = lax.axis_index("clus") * groups
    own_far = lax.dynamic_slice_in_dim(far_list, first, groups, 0)
    own_vec = lax.dynamic_slice_in_dim(far_vector, first, groups, 0)
    incoming = combine_pairs(everyone, table_whole, own_far, own_vec)
    low_real = incoming[:, None, 0] * cosine + incoming[:, None, 1] * sine
    low_imag = incoming[:, None, 1] * cosine - incoming[:, None, 0] * sine
    lowered = jnp.stack([low_real, low_imag], axis=2).reshape(groups * 8, 2, rows_parent, azimuth)
    coarse = jnp.einsum("ab,cqan->cqbn", theta_weights, lowered, precision=highest)
    lower_rim = coarse[:, :, :margin]
    upper_rim = coarse[:, :, coarse.shape[2] - margin :]
    middle = coarse[:, :, margin : coarse.shape[2] - margin]
    from_above = shifted(lower_rim, "samp", -1)
    from_below = shifted(upper_rim, "samp", 1)
    own_rows = middle.shape[2]
    middle = middle.at[:, :, own_rows - margin :].add(from_above)
    middle = middle.at[:, :, :margin].add(from_below)
    child_incoming = jnp.einsum("cqtn,pn->cqtp", middle, phi_matrix, precision=highest)
    return (incoming, child_incoming)


def solution(mesh):
    placed = (
        P("clus", None, "samp", None),
        P(),
        P(),
        P(),
        P(None, "samp", None),
        P(None, None, "samp", "clus"),
        P(),
        P(),
    )
    return jax.shard_map(
        per_device,
        mesh=mesh,
        in_specs=placed,
        out_specs=(P("clus", None, "samp", None), P("clus", None, "samp", None)),
        check_vma=False,
    )
```

profile of v0, /device:TPU:1, one launch (start us, length us, event | category | flops | bytes accessed | tf_op | source)
XLA Modules:
  0.0 659.4 jit_solution(12503561858865681260)
XLA Ops:
  7.2 1.1 copy.97
  8.3 4.9 collective-permute-start
  13.3 5.7 collective-permute-start.1
  19.0 1.6 fusion.24
  21.0 2.9 collective-permute-done.1
  23.8 5.6 fusion.8
  29.5 5.6 fusion
  35.1 0.5 subtract_reduce_fusion.1
  35.9 0.8 copy.107
  37.3 538.4 %all_gather.6 = f32[1024,16,2,6]{1,2,3,0:T(2,128)} all-gather(f32[16,16,2,6]{1,2,3,0:T(2,128)S(1)} %bitcast.74), channel_id=1, replica_groups=mesh['clus'=64,'samp'=8] {'clus'}, dimensions={0}, use_global_device_ids=true | all-gather | bytes 798720 | tf_op jit(solution)/shard_map/all_gather | solution.py:75
  575.7 6.3 copy.94
  582.0 2.4 gather_fusion
  584.4 5.4 copy.96
  589.8 7.6 %gather_fusion.1 = f32[48,2,6,1024]{3,1,2,0:T(2,128)S(1)} fusion(f32[256,2,6,1024]{3,1,2,0:T(2,128)} %all-gather.2.cloned.1.call-done, s32[1024]{0:T(1024)S(1)} %pad_clamp_fusion), kind=kCustom, calls=%fused_computation.1 | custom fusion | bytes 4718784 | tf_op jit(solution)/shard_map/gather | solution.py:40
  597.5 7.3 %subtract_reduce_fusion = (f32[4,6,1024]{2,1,0:T(8,128)S(1)}, f32[4,6,1024]{2,1,0:T(8,128)S(1)}) fusion(f32[4,12,2,6,1024]{4,2,3,1,0:T(2,128)S(1)} %bitcast.65, f32[4,12,2,6,1024]{4,2,3,1,0:T(2,128)} %bitcast.66), kind=kLoop, calls=%fused_computation.26 | loop fusion | flops 2310144 | bytes 4915200 | tf_op jit(solution)/shard_map/reduce_sum | solution.py:44
  604.8 0.3 multiply_add_fusion
  605.1 5.4 fusion.2
  610.4 1.4 copy.125
  612.0 18.1 %collective-permute-start.2 = (f32[32,2,3,1024]{3,0,2,1:T(8,128)S(1)}, f32[32,2,3,1024]{3,0,2,1:T(8,128)S(1)}, u32[]{:S(2)}, u32[]{:S(2)}) collective-permute-start(f32[32,2,3,1024]{3,0,2,1:T(8,128)S(1)} %get-tuple-element.58), channel_id=1, source_target_pairs={{0,7},{1,0},{2,1},{3,2},{4,3},{5,4},{6,5},{7,6},{8,15},{9,8},{10,9... | collective-permute-start | bytes 2359304 | tf_op jit(solution)/shard_map/ppermute | solution.py:27
  630.1 1.9 collective-permute-start.3
  632.3 0.8 copy.112
  633.1 14.6 %collective-permute-done.3 = f32[32,2,3,1024]{3,0,2,1:T(8,128)S(1)} collective-permute-done((f32[32,2,3,1024]{3,0,2,1:T(8,128)S(1)}, f32[32,2,3,1024]{3,0,2,1:T(8,128)S(1)}, u32[]{:S(2)}, u32[]{:S(2)}) %collective-permute-start.3) | collective-permute-done | bytes 786464 | tf_op jit(solution)/shard_map/ppermute | solution.py:27
  647.7 3.8 fusion.6
  651.5 1.1 copy.113
  (35 shorter events, 1.5 us)
Async XLA Ops:
  7.2 22.3 %copy-start = (f32[6,9]{1,0:T(8,128)S(1)}, f32[6,9]{1,0:T(8,128)}, u32[]{:S(2)}) copy-start(f32[6,9]{1,0:T(8,128)} %param.17) | copy-start | bytes 652
  7.2 13.7 %copy-start.2 = (f32[1024,6]{0,1:T(8,128)S(1)}, f32[1024,6]{0,1:T(8,128)}, u32[]{:S(2)}) copy-start(f32[1024,6]{0,1:T(8,128)} %param.19) | copy-start | bytes 73732
  7.2 13.7 %copy-start.3 = (s32[1024,6]{0,1:T(8,128)S(1)}, s32[1024,6]{0,1:T(8,128)}, u32[]{:S(2)}) copy-start(s32[1024,6]{0,1:T(8,128)} %param.18) | copy-start | bytes 73732
  7.2 582.6 %all-gather.2.cloned.1.call-start = ((), (), s32[]{:S(2)}) async-start(), calls=%async_computation | async-start | bytes 12779520 | tf_op jit(solution)/shard_map/all_gather | solution.py:73
  8.3 12.6 %collective-permute-start = (f32[32,2,3,512]{3,0,2,1:T(8,128)S(1)}, f32[32,2,3,512]{3,0,2,1:T(8,128)S(1)}, u32[]{:S(2)}, u32[]{:S(2)}) collective-permute-start(f32[32,2,3,512]{3,0,2,1:T(8,128)S(1)} %copy.97), channel_id=1, source_target_pairs={{0,1},{1,2},{2,3},{3,4},{4,5},{5,6},{6,7},{7,0},{8,9},{9,10},{10,1... | collective-permute-start | bytes 1179656 | tf_op jit(solution)/shard_map/ppermute | solution.py:16
  13.3 10.6 %collective-permute-start.1 = (f32[32,2,3,512]{3,0,2,1:T(8,128)S(1)}, f32[32,2,3,512]{3,0,2,1:T(8,128)S(1)}, u32[]{:S(2)}, u32[]{:S(2)}) collective-permute-start(f32[32,2,3,512]{3,0,2,1:T(8,128)S(1)} %copy.97), channel_id=1, source_target_pairs={{1,0},{2,1},{3,2},{4,3},{5,4},{6,5},{7,6},{0,7},{9,8},{10,9},{11,1... | collective-permute-start | bytes 1179656 | tf_op jit(solution)/shard_map/ppermute | solution.py:18
  35.1 1.6 copy-start.4
  35.1 1.6 copy-start.5
  35.1 2.1 copy-start.1
  612.0 21.1 %collective-permute-start.2 = (f32[32,2,3,1024]{3,0,2,1:T(8,128)S(1)}, f32[32,2,3,1024]{3,0,2,1:T(8,128)S(1)}, u32[]{:S(2)}, u32[]{:S(2)}) collective-permute-start(f32[32,2,3,1024]{3,0,2,1:T(8,128)S(1)} %get-tuple-element.58), channel_id=1, source_target_pairs={{0,7},{1,0},{2,1},{3,2},{4,3},{5,4},{6,5},{7,6},{8,15},{9,8},{10,9... | collective-permute-start | bytes 2359304 | tf_op jit(solution)/shard_map/ppermute | solution.py:27
  630.1 17.5 %collective-permute-start.3 = (f32[32,2,3,1024]{3,0,2,1:T(8,128)S(1)}, f32[32,2,3,1024]{3,0,2,1:T(8,128)S(1)}, u32[]{:S(2)}, u32[]{:S(2)}) collective-permute-start(f32[32,2,3,1024]{3,0,2,1:T(8,128)S(1)} %get-tuple-element.59), channel_id=1, source_target_pairs={{0,1},{1,2},{2,3},{3,4},{4,5},{5,6},{6,7},{7,0},{8,9},{9,10},{10,1... | collective-permute-start | bytes 2359304 | tf_op jit(solution)/shard_map/ppermute | solution.py:27
Sparse Core Ops, SparseCore 0:
  36.8 329.2 all-gather.1
where the time goes:
time: 660 us; the launch traced here: 659 us
  blocking collectives  538 us (82%)
  starting transfers between devices  30.8 us (5%)
  local copies, waits for them, and re-layouts  29.7 us (4%)
  matrix products  20.4 us (3%)
  waiting for transfers between devices  17.5 us (3%)
  between operations  14.3 us (2%)
  other arithmetic  8.32 us (1%)
    all_gather x1, blocking collectives, per_device(): gathered = lax.all_gather(leading, 'clus', axis=0, tiled=True)  538 us
    ppermute x2, starting transfers between devices, shifted(): lax.ppermute(value, axis, [(i, (i + by) % peers) for i in range(peers)])  20.1 us
    ppermute x2, waiting for transfers between devices, shifted(): lax.ppermute(value, axis, [(i, (i + by) % peers) for i in range(peers)])  14.6 us
  transfers between devices with their start and end apart: 5, of which 2 were waited for; matrix products, arithmetic and copies ran while one was open for 3% of the time, Pallas kernels for 0%

commit v1 on v0

v1 whole, which is shorter than its diff:
```python
import jax
import jax.numpy as jnp
from jax import lax
from jax.sharding import PartitionSpec as P

P_SIZE = 6
HIGH = lax.Precision.HIGH


def shifted(value, axis, by):
    peers = lax.axis_size(axis)
    return lax.ppermute(value, axis, [(i, (i + by) % peers) for i in range(peers)])


def phi_table(phi_stencil, phi_weights, columns):
    positions = jnp.arange(columns, dtype=jnp.int32)
    total = jnp.zeros((columns, phi_stencil.shape[0]), jnp.float32)
    for point in range(phi_stencil.shape[1]):
        hits = (phi_stencil[None, :, point] == positions[:, None]).astype(jnp.float32)
        total = total + hits * phi_weights[None, :, point]
    return total


def per_device(
    child_patterns,
    theta_weights,
    phi_stencil,
    phi_weights,
    shift_phase,
    translation_table,
    far_list,
    far_vector,
):
    groups = child_patterns.shape[0] // 8
    columns = child_patterns.shape[3]
    rows_parent = theta_weights.shape[0]
    azimuth = phi_stencil.shape[0]
    margin = P_SIZE // 2
    below = shifted(child_patterns, "samp", 1)
    above = shifted(child_patterns, "samp", -1)
    phi_matrix = phi_table(phi_stencil, phi_weights, columns)
    cosine = jnp.cos(shift_phase)
    sine = jnp.sin(shift_phase)
    extended = jnp.concatenate([below, child_patterns, above], axis=2)
    tilted = jnp.stack(
        [sum(theta_weights[a, b] * extended[:, :, b] for b in range(9)) for a in range(rows_parent)],
        axis=2,
    )
    refined = jnp.einsum("cqap,pn->cqan", tilted, phi_matrix, precision=HIGH)
    refined = refined.reshape(groups, 8, 2, rows_parent, azimuth)
    real_part = refined[:, :, 0] * cosine - refined[:, :, 1] * sine
    imag_part = refined[:, :, 0] * sine + refined[:, :, 1] * cosine
    outgoing = jnp.stack([jnp.sum(real_part, axis=1), jnp.sum(imag_part, axis=1)], axis=1)
    everyone = lax.all_to_all(outgoing, "clus", split_axis=3, concat_axis=0, tiled=True)
    clusters = everyone.shape[0]
    lanes = everyone.shape[2] * everyone.shape[3]
    flat = everyone.reshape(clusters, 2 * lanes)
    table = translation_table.reshape(translation_table.shape[0], 2 * lanes)
    pick = (far_list[:, :, None] == jnp.arange(clusters)[None, None, :]).astype(jnp.float32)
    pick_vec = (far_vector[:, :, None] == jnp.arange(table.shape[0])[None, None, :]).astype(jnp.float32)
    source = jnp.einsum("ilc,cs->lis", pick, flat, precision=HIGH)
    operator = jnp.einsum("ilv,vs->lis", pick_vec, table, precision=HIGH)
    s_re, s_im = source[..., :lanes], source[..., lanes:]
    o_re, o_im = operator[..., :lanes], operator[..., lanes:]
    in_re = jnp.sum(o_re * s_re - o_im * s_im, axis=0)
    in_im = jnp.sum(o_re * s_im + o_im * s_re, axis=0)
    landed = jnp.concatenate([in_re, in_im], axis=1).reshape(everyone.shape)
    incoming = lax.all_to_all(landed, "clus", split_axis=0, concat_axis=3, tiled=True)
    low_real = incoming[:, None, 0] * cosine + incoming[:, None, 1] * sine
    low_imag = incoming[:, None, 1] * cosine - incoming[:, None, 0] * sine
    lowered = jnp.stack([low_real, low_imag], axis=2).reshape(groups * 8, 2, rows_parent, azimuth)
    narrow = jnp.einsum("cqan,pn->cqap", lowered, phi_matrix, precision=HIGH)

    def back(first):
        return jnp.stack(
            [sum(theta_weights[a, b] * narrow[:, :, a] for a in range(rows_parent)) for b in range(first, first + margin)],
            axis=2,
        )

    from_above = shifted(back(0), "samp", -1)
    from_below = shifted(back(2 * margin), "samp", 1)
    child_incoming = back(margin) + from_above + from_below
    return (incoming, child_incoming)


def solution(mesh):
    placed = (
        P("clus", None, "samp", None),
        P(),
        P(),
        P(),
        P(None, "samp", None),
        P(None, None, "samp", "clus"),
        P(),
        P(),
    )
    return jax.shard_map(
        per_device,
        mesh=mesh,
        in_specs=placed,
        out_specs=(P("clus", None, "samp", None), P("clus", None, "samp", None)),
        check_vma=False,
    )
```

time: 660 us -> 208 us (0.32)
  blocking collectives: 538 us -> 24.6 us
  other arithmetic: 8.32 us -> 72.8 us
  local copies, waits for them, and re-layouts: 29.7 us -> 44.1 us
  between operations: 14.3 us -> 1.06 us
  matrix products: 20.4 us -> 9.36 us
    all_gather x1 -> x0, blocking collectives: 538 us -> none  [per_device(): gathered = lax.all_gather(leading, 'clus', axis=0, tiled=True)]
    add x0 -> x10, other arithmetic: none -> 34.6 us  [the longest x9 34.5 us: back(): sum((theta_weights[a, b] * narrow[:, :, a] for a in range(rows_parent)))]
    unnamed x0 -> x5, other arithmetic: none -> 28.8 us
    all_to_all x0 -> x1, blocking collectives: none -> 24.6 us  [per_device(): lax.all_to_all(landed, 'clus', split_axis=0, concat_axis=3, tiled=True)]
    all_to_all x0 -> x1, waiting for transfers between devices: none -> 19.5 us  [per_device(): lax.all_to_all(outgoing, 'clus', split_axis=3, concat_axis=0, tiled=True)]
    unnamed x16 -> x15, local copies, waits for them, and re-layouts: 3.12 us -> 19.8 us
    all_to_all x0 -> x1, starting transfers between devices: none -> 16.5 us  [per_device(): lax.all_to_all(outgoing, 'clus', split_axis=3, concat_axis=0, tiled=True)]
    gather x3 -> x0, local copies, waits for them, and re-layouts: 15.4 us -> none  [the longest x2 7.77 us: combine_pairs(): operator = table[vec_ids]]
  transfers between devices with their start and end apart: 5 -> 5, of which waited for: 2 -> 1; matrix products, arithmetic and copies ran while one was open for 3% -> 9% of each run, Pallas kernels for 0% -> 0%
where the time goes in v1:
time: 208 us; the launch traced here: 207 us
  other arithmetic  72.8 us (35%)
  local copies, waits for them, and re-layouts  44.1 us (21%)
  starting transfers between devices  35.2 us (17%)
  blocking collectives  24.6 us (12%)
  waiting for transfers between devices  19.5 us (9%)
  matrix products  9.36 us (4%)
    add x9, other arithmetic, back(): sum((theta_weights[a, b] * narrow[:, :, a] for a in range(rows_parent)))  34.5 us
    unnamed x5, other arithmetic  28.8 us
    all_to_all x1, blocking collectives, per_device(): lax.all_to_all(landed, 'clus', split_axis=0, concat_axis=3, tiled=True)  24.6 us
    unnamed x15, local copies, waits for them, and re-layouts  19.8 us
    all_to_all x1, waiting for transfers between devices, per_device(): lax.all_to_all(outgoing, 'clus', split_axis=3, concat_axis=0, tiled=True)  19.5 us
    ppermute x4, starting transfers between devices, shifted(): lax.ppermute(value, axis, [(i, (i + by) % peers) for i in range(peers)])  18.8 us
    all_to_all x1, starting transfers between devices, per_device(): lax.all_to_all(outgoing, 'clus', split_axis=3, concat_axis=0, tiled=True)  16.5 us
    all_to_all x2, local copies, waits for them, and re-layouts, per_device(): lax.all_to_all(outgoing, 'clus', split_axis=3, concat_axis=0, tiled=True)  6.5 us
  transfers between devices with their start and end apart: 5, of which 1 were waited for; matrix products, arithmetic and copies ran while one was open for 9% of the time, Pallas kernels for 0%

profile of v1, /device:TPU:1, one launch (start us, length us, event | category | flops | bytes accessed | tf_op | source)
XLA Modules:
  0.0 206.6 jit_solution(3628376807708791519)
XLA Ops:
  1.7 4.9 %collective-permute-start = (f32[32,2,3,512]{3,0,2,1:T(8,128)S(1)}, f32[32,2,3,512]{3,0,2,1:T(8,128)S(1)}, u32[]{:S(2)}, u32[]{:S(2)}) collective-permute-start(f32[32,2,3,512]{3,0,2,1:T(8,128)S(1)} %copy.62), channel_id=1, source_target_pairs={{0,1},{1,2},{2,3},{3,4},{4,5},{5,6},{6,7},{7,0},{8,9},{9,10},{10,1... | collective-permute-start | bytes 1179656 | tf_op jit(solution)/shard_map/ppermute | solution.py:12
  6.6 5.7 %collective-permute-start.1 = (f32[32,2,3,512]{3,0,2,1:T(8,128)S(1)}, f32[32,2,3,512]{3,0,2,1:T(8,128)S(1)}, u32[]{:S(2)}, u32[]{:S(2)}) collective-permute-start(f32[32,2,3,512]{3,0,2,1:T(8,128)S(1)} %copy.62), channel_id=1, source_target_pairs={{0,7},{1,0},{2,1},{3,2},{4,3},{5,4},{6,5},{7,6},{8,15},{9,8},{10,9... | collective-permute-start | bytes 1179656 | tf_op jit(solution)/shard_map/ppermute | solution.py:12
  22.3 5.6 %add_dynamic-update-slice_fusion.5 = f32[32,2,6,512]{3,0,2,1:T(8,128)S(1)} fusion(f32[32,2,3,512]{3,0,2,1:T(8,128)S(1)} %collective-permute-done.1, f32[32,2,3,512]{3,0,2,1:T(8,128)S(1)} %copy.62, f32[32,2,3,512]{3,0,2,1:T(8,128)S(1)} %collective-permute-done, f32[]{:T(128)} %bitcast.9, f32[]{:T(128)} %bitcast.8, f32[]{:T(128)} %bitcast.7, f32[]{:T(128)} %bitcast.6, ...), kind=kLoop, calls=%fused_computation.50 | loop fusion | flops 557055 | bytes 1310756
  27.8 5.8 %add_dynamic-update-slice_fusion.4 = f32[32,2,6,512]{3,0,2,1:T(8,128)S(1)} fusion(f32[32,2,6,512]{3,0,2,1:T(8,128)S(1)} %add_dynamic-update-slice_fusion.5, f32[32,2,3,512]{3,0,2,1:T(8,128)S(1)} %collective-permute-done.1, f32[32,2,3,512]{3,0,2,1:T(8,128)S(1)} %copy.62, f32[32,2,3,512]{3,0,2,1:T(8,128)S(1)} %collective-permute-done, f32[]{:T(128)} %bitcast.18, ...), kind=kLoop, calls=%fused_computation.49 | loop fusion | flops 557056 | bytes 1310756
  33.7 6.0 %add_dynamic-update-slice_fusion.3 = f32[32,2,6,512]{3,0,2,1:T(8,128)S(1)} fusion(f32[32,2,6,512]{3,0,2,1:T(8,128)S(1)} %add_dynamic-update-slice_fusion.4, f32[32,2,3,512]{3,0,2,1:T(8,128)S(1)} %collective-permute-done.1, f32[32,2,3,512]{3,0,2,1:T(8,128)S(1)} %copy.62, f32[32,2,3,512]{3,0,2,1:T(8,128)S(1)} %collective-permute-done, f32[]{:T(128)} %bitcast.27, ...), kind=kLoop, calls=%fused_computation.48 | loop fusion | flops 557056 | bytes 1310756
  39.7 5.6 %add_dynamic-update-slice_fusion.2 = f32[32,2,6,512]{3,0,2,1:T(8,128)S(1)} fusion(f32[32,2,6,512]{3,0,2,1:T(8,128)S(1)} %add_dynamic-update-slice_fusion.3, f32[32,2,3,512]{3,0,2,1:T(8,128)S(1)} %collective-permute-done.1, f32[32,2,3,512]{3,0,2,1:T(8,128)S(1)} %copy.62, f32[32,2,3,512]{3,0,2,1:T(8,128)S(1)} %collective-permute-done, f32[]{:T(128)} %bitcast.36, ...), kind=kLoop, calls=%fused_computation.47 | loop fusion | flops 557056 | bytes 1310756
  45.3 5.8 %add_dynamic-update-slice_fusion.1 = f32[32,2,6,512]{3,0,2,1:T(8,128)S(1)} fusion(f32[32,2,6,512]{3,0,2,1:T(8,128)S(1)} %add_dynamic-update-slice_fusion.2, f32[32,2,3,512]{3,0,2,1:T(8,128)S(1)} %collective-permute-done.1, f32[32,2,3,512]{3,0,2,1:T(8,128)S(1)} %copy.62, f32[32,2,3,512]{3,0,2,1:T(8,128)S(1)} %collective-permute-done, f32[]{:T(128)} %bitcast.45, ...), kind=kLoop, calls=%fused_computation.46 | loop fusion | flops 557056 | bytes 1310756
  51.1 5.7 %add_dynamic-update-slice_fusion = f32[32,2,6,512]{3,0,2,1:T(8,128)S(1)} fusion(f32[32,2,6,512]{3,0,2,1:T(8,128)S(1)} %add_dynamic-update-slice_fusion.1, f32[32,2,3,512]{3,0,2,1:T(8,128)S(1)} %collective-permute-done.1, f32[32,2,3,512]{3,0,2,1:T(8,128)S(1)} %copy.62, f32[32,2,3,512]{3,0,2,1:T(8,128)S(1)} %collective-permute-done, f32[]{:T(128)} %bitcast.54, ...), kind=kLoop, calls=%fused_computation.45 | loop fusion | flops 557056 | bytes 1310756 | tf_op jit(solution)/shard_map/stack | solution.py:45
  63.5 6.6 %reshape.140 = f32[64,1,768]{2,1,0:T(1,128)} reshape(f32[1024,2,4,6]{3,2,1,0:T(4,128)} %bitcast.123) | data formatting | bytes 393216
  70.1 16.5 %all-to-all-start = ((f32[64,1,768]{2,1,0:T(1,128)}), f32[64,1,768]{2,1,0:T(1,128)S(1)}, u32[]{:S(2)}, u32[]{:S(2)}) async-start(f32[64,1,768]{2,1,0:T(1,128)} %reshape.140), calls=%async_computation | async-start | bytes 393216 | tf_op jit(solution)/shard_map/all_to_all | solution.py:54
  87.5 19.5 %all-to-all-done = f32[64,1,768]{2,1,0:T(1,128)S(1)} async-done(((f32[64,1,768]{2,1,0:T(1,128)}), f32[64,1,768]{2,1,0:T(1,128)S(1)}, u32[]{:S(2)}, u32[]{:S(2)}) %all-to-all-start) | async-done | bytes 196640 | tf_op jit(solution)/shard_map/all_to_all | solution.py:54
  108.6 6.8 %reshape.141 = f32[1024,2,4,6]{3,2,1,0:T(4,128)} reshape(f32[64,768]{1,0:T(8,128)S(1)} %reduce) | data formatting | bytes 393216
  115.4 6.0 %copy.80 = f32[4,2,6,64,16]{4,2,1,0,3:T(8,128)} copy(f32[4,2,6,64,16]{2,0,1,4,3:T(4,128)} %bitcast.124) | data formatting | bytes 393216 | tf_op jit(solution)/shard_map/all_to_all | solution.py:54
  130.4 24.6 %all_to_all.33 = f32[64,1,768]{2,1,0:T(1,128)S(1)} all-to-all(f32[64,1,768]{2,1,0:T(1,128)S(1)} %reshape.142), channel_id=1, replica_groups=mesh['clus'=64,'samp'=8] {'clus'}, dimensions={0} | all-to-all | bytes 393216 | tf_op jit(solution)/shard_map/all_to_all | solution.py:68
  162.8 3.9 %multiply_add_fusion.3 = f32[32,2,1,512]{3,0,2,1:T(8,128)S(1)} fusion(f32[32,2,6,512]{3,0,2,1:T(8,128)S(1)} %fusion.1, f32[]{:T(128)} %bitcast.48, f32[]{:T(128)} %bitcast.39, f32[]{:T(128)} %bitcast.30, f32[]{:T(128)} %bitcast.21, f32[]{:T(128)} %bitcast.12, f32[]{:T(128)} %bitcast.3), kind=kLoop, calls=%fused_computation.39 | loop fusion | flops 360448 | bytes 917528 | tf_op jit(solution)/shard_map/add | solution.py:76
  166.7 3.9 %multiply_add_fusion.4 = f32[32,2,1,512]{3,0,2,1:T(8,128)S(1)} fusion(f32[32,2,6,512]{3,0,2,1:T(8,128)S(1)} %fusion.1, f32[]{:T(128)} %bitcast.47, f32[]{:T(128)} %bitcast.38, f32[]{:T(128)} %bitcast.29, f32[]{:T(128)} %bitcast.20, f32[]{:T(128)} %bitcast.11, f32[]{:T(128)} %bitcast.2), kind=kLoop, calls=%fused_computation.40 | loop fusion | flops 360448 | bytes 917528 | tf_op jit(solution)/shard_map/add | solution.py:76
  170.6 4.1 %multiply_add_fusion.5 = f32[32,2,1,512]{3,0,2,1:T(8,128)S(1)} fusion(f32[32,2,6,512]{3,0,2,1:T(8,128)S(1)} %fusion.1, f32[]{:T(128)} %bitcast.46, f32[]{:T(128)} %bitcast.37, f32[]{:T(128)} %bitcast.28, f32[]{:T(128)} %bitcast.19, f32[]{:T(128)} %bitcast.10, f32[]{:T(128)} %bitcast.1), kind=kLoop, calls=%fused_computation.41 | loop fusion | flops 360448 | bytes 917528 | tf_op jit(solution)/shard_map/add | solution.py:76
  174.7 3.6 %multiply_add_fusion.1 = f32[32,2,1,512]{3,0,2,1:T(8,128)S(1)} fusion(f32[32,2,6,512]{3,0,2,1:T(8,128)S(1)} %fusion.1, f32[]{:T(128)} %bitcast.53, f32[]{:T(128)} %bitcast.44, f32[]{:T(128)} %bitcast.35, f32[]{:T(128)} %bitcast.26, f32[]{:T(128)} %bitcast.17, f32[]{:T(128)} %bitcast.8), kind=kLoop, calls=%fused_computation.37 | loop fusion | flops 360448 | bytes 917528 | tf_op jit(solution)/shard_map/add | solution.py:76
  178.4 3.7 %multiply_add_fusion.2 = f32[32,2,1,512]{3,0,2,1:T(8,128)S(1)} fusion(f32[32,2,6,512]{3,0,2,1:T(8,128)S(1)} %fusion.1, f32[]{:T(128)} %bitcast.52, f32[]{:T(128)} %bitcast.43, f32[]{:T(128)} %bitcast.34, f32[]{:T(128)} %bitcast.25, f32[]{:T(128)} %bitcast.16, f32[]{:T(128)} %bitcast.7), kind=kLoop, calls=%fused_computation.38 | loop fusion | flops 360448 | bytes 917528 | tf_op jit(solution)/shard_map/add | solution.py:76
  182.1 3.8 %multiply_add_fusion = f32[32,2,1,512]{3,0,2,1:T(8,128)S(1)} fusion(f32[32,2,6,512]{3,0,2,1:T(8,128)S(1)} %fusion.1, f32[]{:T(128)} %bitcast.54, f32[]{:T(128)} %bitcast.45, f32[]{:T(128)} %bitcast.36, f32[]{:T(128)} %bitcast.27, f32[]{:T(128)} %bitcast.18, f32[]{:T(128)} %bitcast.9), kind=kLoop, calls=%fused_computation.36 | loop fusion | flops 360448 | bytes 917528 | tf_op jit(solution)/shard_map/add | solution.py:76
  185.9 3.6 %multiply_add_fusion.6 = f32[32,2,1,512]{3,0,2,1:T(8,128)S(1)} fusion(f32[32,2,6,512]{3,0,2,1:T(8,128)S(1)} %fusion.1, f32[]{:T(128)} %bitcast.51, f32[]{:T(128)} %bitcast.42, f32[]{:T(128)} %bitcast.33, f32[]{:T(128)} %bitcast.24, f32[]{:T(128)} %bitcast.15, f32[]{:T(128)} %bitcast.6), kind=kLoop, calls=%fused_computation.42 | loop fusion | flops 360448 | bytes 917528 | tf_op jit(solution)/shard_map/add | solution.py:76
  189.6 5.3 %collective-permute-start.2 = (f32[32,2,3,512]{3,0,2,1:T(8,128)S(1)}, f32[32,2,3,512]{3,0,2,1:T(8,128)S(1)}, u32[]{:S(2)}, u32[]{:S(2)}) collective-permute-start(f32[32,2,3,512]{3,0,2,1:T(8,128)S(1)} %pad_maximum_fusion), channel_id=1, source_target_pairs={{0,7},{1,0},{2,1},{3,2},{4,3},{5,4},{6,5},{7,6},{8,15},{9,8},{10,9... | collective-permute-start | bytes 1179656 | tf_op jit(solution)/shard_map/ppermute | solution.py:12
  197.7 3.8 %multiply_add_fusion.7 = f32[32,2,1,512]{3,0,2,1:T(8,128)S(1)} fusion(f32[32,2,6,512]{3,0,2,1:T(8,128)S(1)} %fusion.1, f32[]{:T(128)} %bitcast.50, f32[]{:T(128)} %bitcast.41, f32[]{:T(128)} %bitcast.32, f32[]{:T(128)} %bitcast.23, f32[]{:T(128)} %bitcast.14, f32[]{:T(128)} %bitcast.5), kind=kLoop, calls=%fused_computation.43 | loop fusion | flops 360448 | bytes 917528 | tf_op jit(solution)/shard_map/add | solution.py:76
  201.5 3.9 %multiply_add_fusion.8 = f32[32,2,1,512]{3,0,2,1:T(8,128)S(1)} fusion(f32[32,2,6,512]{3,0,2,1:T(8,128)S(1)} %fusion.1, f32[]{:T(128)} %bitcast.49, f32[]{:T(128)} %bitcast.40, f32[]{:T(128)} %bitcast.31, f32[]{:T(128)} %bitcast.22, f32[]{:T(128)} %bitcast.13, f32[]{:T(128)} %bitcast.4), kind=kLoop, calls=%fused_computation.44 | loop fusion | flops 360448 | bytes 917528 | tf_op jit(solution)/shard_map/add | solution.py:76
  (48 shorter events, 40.7 us)
Async XLA Ops:
  1.7 20.5 %collective-permute-start = (f32[32,2,3,512]{3,0,2,1:T(8,128)S(1)}, f32[32,2,3,512]{3,0,2,1:T(8,128)S(1)}, u32[]{:S(2)}, u32[]{:S(2)}) collective-permute-start(f32[32,2,3,512]{3,0,2,1:T(8,128)S(1)} %copy.62), channel_id=1, source_target_pairs={{0,1},{1,2},{2,3},{3,4},{4,5},{5,6},{6,7},{7,0},{8,9},{9,10},{10,1... | collective-permute-start | bytes 1179656 | tf_op jit(solution)/shard_map/ppermute | solution.py:12
  6.6 15.6 %collective-permute-start.1 = (f32[32,2,3,512]{3,0,2,1:T(8,128)S(1)}, f32[32,2,3,512]{3,0,2,1:T(8,128)S(1)}, u32[]{:S(2)}, u32[]{:S(2)}) collective-permute-start(f32[32,2,3,512]{3,0,2,1:T(8,128)S(1)} %copy.62), channel_id=1, source_target_pairs={{0,7},{1,0},{2,1},{3,2},{4,3},{5,4},{6,5},{7,6},{8,15},{9,8},{10,9... | collective-permute-start | bytes 1179656 | tf_op jit(solution)/shard_map/ppermute | solution.py:12
  63.5 23.1 %copy-start.1 = (f32[16,2,6,16]{3,1,2,0:T(2,128)S(1)}, f32[16,2,6,16]{3,1,2,0:T(2,128)}, u32[]{:S(2)}) copy-start(f32[16,2,6,16]{3,1,2,0:T(2,128)} %param.13) | copy-start | bytes 36868
  63.5 23.2 %copy-start.2 = (s32[256,12]{0,1:T(8,128)S(1)}, s32[256,12]{0,1:T(8,128)}, u32[]{:S(2)}) copy-start(s32[256,12]{0,1:T(8,128)} %param.15) | copy-start | bytes 36868
  70.1 36.9 %all-to-all-start = ((f32[64,1,768]{2,1,0:T(1,128)}), f32[64,1,768]{2,1,0:T(1,128)S(1)}, u32[]{:S(2)}, u32[]{:S(2)}) async-start(f32[64,1,768]{2,1,0:T(1,128)} %reshape.140), calls=%async_computation | async-start | bytes 393216 | tf_op jit(solution)/shard_map/all_to_all | solution.py:54
  121.4 2.4 %copy-start.3 = (s32[256,12]{0,1:T(8,128)S(1)}, s32[256,12]{0,1:T(8,128)}, u32[]{:S(2)}) copy-start(s32[256,12]{0,1:T(8,128)} %param.14) | copy-start | bytes 36868
  159.4 3.3 %copy-start = (f32[4,2,6,1024]{3,1,2,0:T(2,128)}, f32[4,2,6,1024]{3,1,2,0:T(2,128)S(1)}, u32[]{:S(2)}) copy-start(f32[4,2,6,1024]{3,1,2,0:T(2,128)S(1)} %all_to_all.30) | copy-start | bytes 589828
  189.6 15.9 %collective-permute-start.2 = (f32[32,2,3,512]{3,0,2,1:T(8,128)S(1)}, f32[32,2,3,512]{3,0,2,1:T(8,128)S(1)}, u32[]{:S(2)}, u32[]{:S(2)}) collective-permute-start(f32[32,2,3,512]{3,0,2,1:T(8,128)S(1)} %pad_maximum_fusion), channel_id=1, source_target_pairs={{0,7},{1,0},{2,1},{3,2},{4,3},{5,4},{6,5},{7,6},{8,15},{9,8},{10,9... | collective-permute-start | bytes 1179656 | tf_op jit(solution)/shard_map/ppermute | solution.py:12
  194.9 10.6 %collective-permute-start.3 = (f32[32,2,3,512]{3,0,2,1:T(8,128)S(1)}, f32[32,2,3,512]{3,0,2,1:T(8,128)S(1)}, u32[]{:S(2)}, u32[]{:S(2)}) collective-permute-start(f32[32,2,3,512]{3,0,2,1:T(8,128)S(1)} %pad_maximum_fusion.1), channel_id=1, source_target_pairs={{0,1},{1,2},{2,3},{3,4},{4,5},{5,6},{6,7},{7,0},{8,9},{9,10},{10,1... | collective-permute-start | bytes 1179656 | tf_op jit(solution)/shard_map/ppermute | solution.py:12

commit v2 on v1

v2 whole, which is shorter than its diff:
```python
import functools

import jax
import jax.numpy as jnp
from jax import lax
from jax.experimental import pallas as pl
from jax.experimental.pallas import tpu as pltpu
from jax.sharding import PartitionSpec as P

MESH = pl.DeviceIdType.MESH
F32 = jnp.float32
BF16 = jnp.bfloat16


def halves(value):
    high = value.astype(BF16)
    return high, (value - high.astype(F32)).astype(BF16)


def dot(a, b, contract):
    return lax.dot_general(a, b, ((contract[0], contract[1]), ((), ())), preferred_element_type=F32)


def dot3(a_hi, a_lo, b_hi, b_lo, contract):
    return dot(a_hi, b_hi, contract) + (dot(a_hi, b_lo, contract) + dot(a_lo, b_hi, contract))


def window(
    n_clus, n_samp,
    theta, child, stencil, weights, phase, table, far, vec,
    inc_out, child_out,
    phi_hi, phi_lo, cosine, sine, picks, operators,
    below, above, lhs_hi, lhs_lo, low_hi, low_lo,
    msg_out, msg_in, back_out, back_in, rim_low, rim_high, got_above, got_below,
    halo_send, halo_recv, a2a_send, a2a_recv, own_sem, back_send, back_recv, rim_send, rim_recv,
):
    me = lax.axis_index("clus")
    ring = lax.axis_index("samp")
    up = lax.rem(ring + 1, n_samp)
    down = lax.rem(ring + n_samp - 1, n_samp)
    columns = child.shape[2]
    azimuth = stencil.shape[1]
    rows = phase.shape[1]
    far_count = far.shape[1]
    blocks = azimuth // 128
    per_block = n_clus // blocks
    width = 128 // per_block

    barrier = pltpu.get_barrier_semaphore()
    for side in (up, down):
        pl.semaphore_signal(barrier, inc=1, device_id=(me, side), device_id_type=MESH)

    def greet(step, carry):
        pl.semaphore_signal(barrier, inc=1, device_id=(lax.rem(me + step, n_clus), ring), device_id_type=MESH)
        return carry

    lax.fori_loop(1, n_clus, greet, 0)

    def build(step, carry):
        first = pl.multiple_of(step * 32, 32)
        places = lax.broadcasted_iota(jnp.int32, (32, azimuth), 0) + first
        total = jnp.zeros((32, azimuth), F32)
        for point in range(stencil.shape[0]):
            total = total + jnp.where(stencil[point : point + 1, :] == places, weights[point : point + 1, :], 0.0)
        high, low = halves(total)
        phi_hi[pl.ds(first, 32), :] = high
        phi_lo[pl.ds(first, 32), :] = low
        return carry

    lax.fori_loop(0, columns // 32, build, 0)

    pl.semaphore_wait(barrier, n_clus + 1)
    halos = [
        pltpu.make_async_remote_copy(
            src_ref=child, dst_ref=below, send_sem=halo_send.at[0], recv_sem=halo_recv.at[0],
            device_id=(me, up), device_id_type=MESH,
        ),
        pltpu.make_async_remote_copy(
            src_ref=child, dst_ref=above, send_sem=halo_send.at[1], recv_sem=halo_recv.at[1],
            device_id=(me, down), device_id_type=MESH,
        ),
    ]
    for copy in halos:
        copy.start()

    for octant in range(8):
        angle = phase[octant]
        cosine[octant] = jnp.cos(angle)
        sine[octant] = jnp.sin(angle)

    clusters = far.shape[0]
    t_hi, t_lo = halves(table[...])
    places = lax.broadcasted_iota(jnp.int32, (clusters, clusters), 1)
    kinds = lax.broadcasted_iota(jnp.int32, (clusters, table.shape[0]), 1)
    for link in range(far_count):
        picks[link] = jnp.where(far[:, link : link + 1] == places, 1.0, 0.0).astype(BF16)
        chosen = jnp.where(vec[:, link : link + 1] == kinds, 1.0, 0.0).astype(BF16)
        operators[link] = dot(chosen, t_hi, ((1,), (0,))) + dot(chosen, t_lo, ((1,), (0,)))

    for copy in halos:
        copy.wait()

    for row in range(rows):
        total = jnp.zeros((64, columns), F32)
        for step in range(9):
            part = (below, child, above)[step // 3][step % 3]
            total = total + theta[row, step] * part
        high, low = halves(total)
        lhs_hi[row * 64 : (row + 1) * 64, :] = high
        lhs_lo[row * 64 : (row + 1) * 64, :] = low

    half = lax.broadcasted_iota(jnp.int32, (8, 128), 0) < 4
    group = lax.broadcasted_iota(jnp.int32, (8, 128), 1) // width

    for block in range(blocks):
        lanes = slice(block * 128, (block + 1) * 128)
        refined = dot3(lhs_hi[...], lhs_lo[...], phi_hi[:, lanes], phi_lo[:, lanes], ((1,), (0,)))
        fields = []
        for row in range(rows):
            straight = jnp.zeros((8, 128), F32)
            crossed = jnp.zeros((8, 128), F32)
            for octant in range(8):
                piece = refined[row * 64 + octant * 8 : row * 64 + octant * 8 + 8]
                straight = straight + piece * cosine[octant, row : row + 1, lanes]
                crossed = crossed + piece * sine[octant, row : row + 1, lanes]
            crossed = pltpu.roll(crossed, 4, 0)
            fields.append(straight + jnp.where(half, -crossed, crossed))
        for part in range(per_block):
            packed = jnp.zeros((8, 128), F32)
            for row in range(rows):
                moved = pltpu.roll(fields[row], ((row - part) * width) % 128, 1)
                packed = jnp.where(group == row, moved, packed)
            msg_out[block * per_block + part] = packed
        for part in range(per_block):
            target = block * per_block + part

            @pl.when(target != me)
            def _():
                pltpu.make_async_remote_copy(
                    src_ref=msg_out.at[target], dst_ref=msg_in.at[me], send_sem=a2a_send, recv_sem=a2a_recv,
                    device_id=(target, ring), device_id_type=MESH,
                ).start()

    own = pltpu.make_async_copy(msg_out.at[me], msg_in.at[me], own_sem.at[0])
    own.start()
    own.wait()
    others = pl.ds(0, n_clus - 1)
    pltpu.make_async_copy(msg_out.at[others], msg_in.at[others], a2a_recv).wait()

    pairs = n_clus // 2
    arrived = msg_in[...].reshape(pairs, 2, 8, 128)
    even, odd = arrived[:, 0], arrived[:, 1]
    half_b = lax.broadcasted_iota(jnp.int32, (pairs, 8, 128), 1) < 4
    real = jnp.where(half_b, even, pltpu.roll(odd, 4, 1)).reshape(clusters, 128)
    imag = jnp.where(half_b, pltpu.roll(even, 4, 1), odd).reshape(clusters, 128)
    x_hi, x_lo = halves(jnp.concatenate([real, imag], axis=1))
    in_re = jnp.zeros((clusters, 128), F32)
    in_im = jnp.zeros((clusters, 128), F32)
    for link in range(far_count):
        pick = picks[link]
        source = dot(pick, x_hi, ((1,), (0,))) + dot(pick, x_lo, ((1,), (0,)))
        s_re, s_im = source[:, :128], source[:, 128:]
        o_re, o_im = operators[link, :, :128], operators[link, :, 128:]
        in_re = in_re + (o_re * s_re - o_im * s_im)
        in_im = in_im + (o_re * s_im + o_im * s_re)
    in_re = in_re.reshape(pairs, 8, 128)
    in_im = in_im.reshape(pairs, 8, 128)
    back_even = jnp.where(half_b, in_re, pltpu.roll(in_im, 4, 1))
    back_odd = jnp.where(half_b, pltpu.roll(in_re, 4, 1), in_im)
    back_out[...] = jnp.stack([back_even, back_odd], axis=1).reshape(n_clus, 8, 128)

    def give(step, carry):
        target = lax.rem(me + step, n_clus)
        pltpu.make_async_remote_copy(
            src_ref=back_out.at[target], dst_ref=back_in.at[me], send_sem=back_send, recv_sem=back_recv,
            device_id=(target, ring), device_id_type=MESH,
        ).start()
        return carry

    lax.fori_loop(1, n_clus, give, 0)
    own = pltpu.make_async_copy(back_out.at[me], back_in.at[me], own_sem.at[1])
    own.start()
    own.wait()
    pltpu.make_async_copy(back_out.at[others], back_in.at[others], back_recv).wait()

    for block in range(blocks):
        lanes = slice(block * 128, (block + 1) * 128)
        for row in range(rows):
            field = jnp.zeros((8, 128), F32)
            for part in range(per_block):
                moved = pltpu.roll(back_in[block * per_block + part], ((part - row) * width) % 128, 1)
                field = jnp.where(group == part, moved, field)
            inc_out[row, :, lanes] = field
            swapped = pltpu.roll(field, 4, 0)
            swapped = jnp.where(half, swapped, -swapped)
            for octant in range(0, 8, 2):
                pieces = [
                    field * cosine[o, row : row + 1, lanes] + swapped * sine[o, row : row + 1, lanes]
                    for o in (octant, octant + 1)
                ]
                high, low = halves(jnp.concatenate(pieces, axis=0))
                low_hi[row * 64 + octant * 8 : row * 64 + octant * 8 + 16, lanes] = high
                low_lo[row * 64 + octant * 8 : row * 64 + octant * 8 + 16, lanes] = low

    for cut in range(0, columns, 256):
        span = slice(cut, cut + 256)
        narrow = dot3(low_hi[...], low_lo[...], phi_hi[span, :], phi_lo[span, :], ((1,), (1,)))
        for step in range(9):
            total = jnp.zeros((64, 256), F32)
            for row in range(rows):
                total = total + theta[row, step] * narrow[row * 64 : (row + 1) * 64]
            (rim_low, child_out, rim_high)[step // 3][step % 3, :, span] = total

    rims = [
        pltpu.make_async_remote_copy(
            src_ref=rim_low, dst_ref=got_above, send_sem=rim_send.at[0], recv_sem=rim_recv.at[0],
            device_id=(me, down), device_id_type=MESH,
        ),
        pltpu.make_async_remote_copy(
            src_ref=rim_high, dst_ref=got_below, send_sem=rim_send.at[1], recv_sem=rim_recv.at[1],
            device_id=(me, up), device_id_type=MESH,
        ),
    ]
    for copy in rims:
        copy.start()
    pltpu.make_async_copy(msg_out.at[others], msg_in.at[others], a2a_send).wait()
    pltpu.make_async_copy(back_out.at[others], back_in.at[others], back_send).wait()
    for copy in rims:
        copy.wait()
    child_out[...] = child_out[...] + got_above[...] + got_below[...]


def per_device(n_clus, n_samp, child_patterns, theta_weights, phi_stencil, phi_weights, shift_phase, translation_table, far_list, far_vector):
    groups = child_patterns.shape[0] // 8
    own_rows, columns = child_patterns.shape[2:]
    rows = theta_weights.shape[0]
    azimuth = phi_stencil.shape[0]
    clusters, far_count = far_list.shape
    kinds = translation_table.shape[0]
    child = child_patterns.reshape(groups, 8, 2, own_rows, columns).transpose(3, 1, 2, 0, 4)
    child = child.reshape(own_rows, groups * 16, columns)
    lanes = rows * translation_table.shape[3]
    table = jnp.pad(translation_table.reshape(kinds, 2, lanes), ((0, 0), (0, 0), (0, 128 - lanes)))
    table = table.reshape(kinds, 256)
    vmem = pl.BlockSpec(memory_space=pltpu.VMEM)
    smem = pl.BlockSpec(memory_space=pltpu.SMEM)
    block = (own_rows, groups * 16, columns)
    incoming, child_incoming = pl.pallas_call(
        functools.partial(window, n_clus, n_samp),
        out_shape=(
            jax.ShapeDtypeStruct((rows, 8, azimuth), F32),
            jax.ShapeDtypeStruct(block, F32),
        ),
        in_specs=[smem] + [vmem] * 7,
        out_specs=(vmem, vmem),
        scratch_shapes=[
            pltpu.VMEM((columns, azimuth), BF16),
            pltpu.VMEM((columns, azimuth), BF16),
            pltpu.VMEM((8, rows, azimuth), F32),
            pltpu.VMEM((8, rows, azimuth), F32),
            pltpu.VMEM((far_count, clusters, clusters), BF16),
            pltpu.VMEM((far_count, clusters, 256), F32),
            pltpu.VMEM(block, F32),
            pltpu.VMEM(block, F32),
            pltpu.VMEM((rows * 64, columns), BF16),
            pltpu.VMEM((rows * 64, columns), BF16),
            pltpu.VMEM((rows * 64, azimuth), BF16),
            pltpu.VMEM((rows * 64, azimuth), BF16),
            pltpu.VMEM((n_clus, 8, 128), F32),
            pltpu.VMEM((n_clus, 8, 128), F32),
            pltpu.VMEM((n_clus, 8, 128), F32),
            pltpu.VMEM((n_clus, 8, 128), F32),
            pltpu.VMEM(block, F32),
            pltpu.VMEM(block, F32),
            pltpu.VMEM(block, F32),
            pltpu.VMEM(block, F32),
            pltpu.SemaphoreType.DMA((2,)),
            pltpu.SemaphoreType.DMA((2,)),
            pltpu.SemaphoreType.DMA,
            pltpu.SemaphoreType.DMA,
            pltpu.SemaphoreType.DMA((2,)),
            pltpu.SemaphoreType.DMA,
            pltpu.SemaphoreType.DMA,
            pltpu.SemaphoreType.DMA((2,)),
            pltpu.SemaphoreType.DMA((2,)),
        ],
        compiler_params=pltpu.CompilerParams(collective_id=0, has_side_effects=True, vmem_limit_bytes=48 << 20),
    )(theta_weights, child, phi_stencil.T, phi_weights.T, shift_phase, table, far_list, far_vector)
    incoming = incoming.reshape(rows, 2, groups, azimuth).transpose(2, 1, 0, 3)
    child_incoming = child_incoming.reshape(own_rows, 8, 2, groups, columns).transpose(3, 1, 2, 0, 4)
    return incoming, child_incoming.reshape(child_patterns.shape)


def solution(mesh):
    placed = (
        P("clus", None, "samp", None),
        P(),
        P(),
        P(),
        P(None, "samp", None),
        P(None, None, "samp", "clus"),
        P(),
        P(),
    )
    return jax.shard_map(
        functools.partial(per_device, mesh.shape["clus"], mesh.shape["samp"]),
        mesh=mesh,
        in_specs=placed,
        out_specs=(P("clus", None, "samp", None), P("clus", None, "samp", None)),
        check_vma=False,
    )
```

time: 208 us -> 85.4 us (0.41)
  the two profiles are of different devices: /device:TPU:1 before, /device:TPU:6 now
where the time goes in v2:
time: 85.4 us; the launch traced here: 85.1 us
  Pallas kernels  79.3 us (93%)
  local copies, waits for them, and re-layouts  5.05 us (6%)
    pallas_call x1, Pallas kernels, per_device(): pl.pallas_call(functools.partial(window, n_clus, n_samp), out_shape=(jax....  79.3 us
    unnamed x20, local copies, waits for them, and re-layouts  2.7 us

profile of v2, /device:TPU:6, one launch (start us, length us, event | category | flops | bytes accessed | tf_op | source)
XLA Modules:
  0.0 85.1 jit_solution(791822714441648628)
XLA Ops:
  0.6 0.9 %copy.25 = f32[16,2,6,16]{3,2,1,0:T(8,128)S(1)} copy(f32[16,2,6,16]{3,1,2,0:T(2,128)} %param.13) | data formatting | bytes 24576
  1.5 0.0 copy-start.5
  1.6 0.1 reshape.32
  1.7 0.0 copy-start.6
  1.7 0.0 copy-start.4
  1.7 0.0 copy-start.3
  1.7 0.5 copy-done.5
  2.3 0.1 copy.20.far
  2.4 0.1 copy.21.vec
  2.5 0.1 copy-done.4
  2.6 0.1 copy.19.phase
  2.7 0.1 copy-done.3
  2.8 0.3 copy.31
  3.0 0.0 copy-start
  3.1 0.0 copy-start.1
  3.1 0.0 copy-start.2
  3.1 0.1 reshape.26.child
  3.2 0.6 copy-done
  3.8 0.0 copy-done.1
  3.8 79.3 %shard_map.95 = (f32[6,8,1024]{2,1,0:T(8,128)S(1)}, f32[3,64,512]{2,1,0:T(8,128)S(1)}) custom-call(f32[6,9]{1,0:T(8,128)S(1)} %copy-done.2, f32[3,64,512]{2,1,0:T(8,128)S(1)} %reshape.26.child, s32[6,1024]{1,0:T(8,128)S(1)} %bitcast.16, f32[6,1024]{1,0:T(8,128)S(1)} %bitcast.17, f32[8,6,1024]{2,1,0:T(8,128)S(1)} %copy.19.phase, f32[16,256]{1,0:T(8,128)S(1)} %bitcast.15, ...), custom_call_target="tpu_custom_call" | custom-call | tf_op jit(solution)/shard_map/pallas_call | solution.py:248
  83.1 0.1 reshape.29
  83.2 0.8 copy.32
  84.0 0.1 reshape.30
  84.2 0.9 %copy.23 = f32[4,8,2,3,512]{4,2,3,1,0:T(2,128)} copy(f32[4,8,2,3,512]{4,0,2,1,3:T(4,128)S(1)} %bitcast.18) | data formatting | bytes 786432 | tf_op jit(solution)/shard_map/transpose | solution.py:290
  (4 shorter events, 0.0 us)
Async XLA Ops:
  1.5 0.7 copy-start.5
  1.7 0.7 copy-start.6
  1.7 0.9 %copy-start.4 = (f32[8,6,1024]{2,0,1:T(8,128)S(1)}, f32[8,6,1024]{2,0,1:T(8,128)}, u32[]{:S(2)}) copy-start(f32[8,6,1024]{2,0,1:T(8,128)} %param.12) | copy-start | bytes 589828
  1.7 1.1 %copy-start.3 = (f32[32,2,3,512]{3,1,2,0:T(2,128)S(1)}, f32[32,2,3,512]{3,1,2,0:T(2,128)}, u32[]{:S(2)}) copy-start(f32[32,2,3,512]{3,1,2,0:T(2,128)} %param.8) | copy-start | bytes 1179652
  3.0 0.8 copy-start
  3.1 0.8 copy-start.1
  3.1 0.8 copy-start.2

commit v3 on v2

v3 whole, which is shorter than its diff:
```python
import functools

import jax
import jax.numpy as jnp
from jax import lax
from jax.experimental import pallas as pl
from jax.experimental.pallas import tpu as pltpu
from jax.sharding import PartitionSpec as P

MESH = pl.DeviceIdType.MESH
F32 = jnp.float32
BF16 = jnp.bfloat16


def halves(value):
    high = value.astype(BF16)
    return high, (value - high.astype(F32)).astype(BF16)


def dot(a, b, contract):
    return lax.dot_general(a, b, ((contract[0], contract[1]), ((), ())), preferred_element_type=F32)


def dot3(a_hi, a_lo, b_hi, b_lo, contract):
    return dot(a_hi, b_hi, contract) + (dot(a_hi, b_lo, contract) + dot(a_lo, b_hi, contract))


def swap_groups(value):
    row = lax.broadcasted_iota(jnp.int32, (8, 128), 0)
    group = lax.broadcasted_iota(jnp.int32, (8, 128), 1) // 16
    for bit in (4, 2, 1):
        own, other = (row // bit) % 2, (group // bit) % 2
        rise = pltpu.roll(pltpu.roll(value, 8 - bit, 1), 16 * bit, 2)
        fall = rise if bit == 4 else pltpu.roll(pltpu.roll(value, bit, 1), 128 - 16 * bit, 2)
        value = jnp.where((own == other)[None], value, jnp.where((own < other)[None], rise, fall))
    return value


def window(
    n_clus, n_samp,
    theta, child, stencil_in, weights_in, phase_in, table_in, far_in, vec_in,
    inc_out, child_out,
    stencil, weights, phase, table, far, vec,
    phi_hi, phi_lo, cosine, sine, picks, operators,
    below, above, lhs_hi, lhs_lo, low_hi, low_lo, total_low,
    msg_out, msg_in, back_out, back_in, inc_pair, inc_far,
    in_sem, halo_send, halo_recv, phase_send, phase_recv,
    a2a_send, a2a_recv, own_sem, back_send, back_recv, inc_send, inc_recv,
):
    me = lax.axis_index("clus")
    ring = lax.axis_index("samp")
    up = lax.rem(ring + 1, n_samp)
    down = lax.rem(ring + n_samp - 1, n_samp)
    core = lax.rem(ring, 2)
    pair = ring + 1 - 2 * core
    away = lax.rem(ring + n_samp - 1 + 2 * core, n_samp)
    deep = lax.rem(lax.div(me, 4), 4)
    first_end = jnp.where(ring == 0, 3, 0)
    last_end = jnp.where(ring == n_samp - 1, 1, 0)
    near = me + 4 * (lax.rem(deep + first_end + last_end, 4) - deep)
    columns = child.shape[2]
    azimuth = stencil.shape[1]
    rows = phase.shape[0]
    far_count, clusters = far.shape
    others = pl.ds(0, n_clus - 1)

    loads = [
        pltpu.make_async_copy(source, target, in_sem.at[place])
        for place, (source, target) in enumerate(
            [(stencil_in, stencil), (weights_in, weights), (phase_in, phase), (table_in, table), (far_in, far), (vec_in, vec)]
        )
    ]
    for copy in loads:
        copy.start()

    barrier = pltpu.get_barrier_semaphore()
    for peer in ((me, up), (me, down), (near, away)):
        pl.semaphore_signal(barrier, inc=1, device_id=peer, device_id_type=MESH)

    def greet(step, carry):
        pl.semaphore_signal(barrier, inc=1, device_id=(lax.rem(me + step, n_clus), ring), device_id_type=MESH)
        return carry

    lax.fori_loop(1, n_clus, greet, 0)

    loads[0].wait()
    loads[1].wait()

    def build(step, carry):
        first = pl.multiple_of(step * 32, 32)
        places = lax.broadcasted_iota(jnp.int32, (32, azimuth), 0) + first
        total = jnp.zeros((32, azimuth), F32)
        for point in range(stencil.shape[0]):
            total = total + jnp.where(stencil[point : point + 1, :] == places, weights[point : point + 1, :], 0.0)
        high, low = halves(total)
        phi_hi[pl.ds(first, 32), :] = high
        phi_lo[pl.ds(first, 32), :] = low
        return carry

    lax.fori_loop(0, columns // 32, build, 0)
    for copy in loads[2:]:
        copy.wait()

    pl.semaphore_wait(barrier, n_clus + 2)
    halos = [
        pltpu.make_async_remote_copy(
            src_ref=child, dst_ref=target, send_sem=halo_send.at[place], recv_sem=halo_recv.at[place],
            device_id=(me, side), device_id_type=MESH,
        )
        for place, (target, side) in enumerate([(below, up), (above, down)])
    ]
    for copy in halos:
        copy.start()
    tilts = [
        pltpu.make_async_remote_copy(
            src_ref=phase, dst_ref=cosine.at[place], send_sem=phase_send.at[place - 1], recv_sem=phase_recv.at[place - 1],
            device_id=peer, device_id_type=MESH,
        )
        for place, peer in ((1, (me, pair)), (2, (near, away)))
    ]
    for copy in tilts:
        copy.start()

    for row in range(rows):
        cosine[0, row] = jnp.cos(phase[row])
        sine[0, row] = jnp.sin(phase[row])

    inner = clusters // n_clus
    spot = lax.broadcasted_iota(jnp.int32, (clusters, clusters), 0)
    lane = lax.broadcasted_iota(jnp.int32, (clusters, clusters), 1)
    order = jnp.where((spot % n_clus) * inner + spot // n_clus == lane, 1.0, 0.0).astype(BF16)
    partner = far[...]
    partner = (partner % inner) * n_clus + partner // inner
    wanted = dot(order, partner.astype(F32).astype(BF16), ((1,), (1,)))
    kinds = dot(order, vec[...].astype(F32).astype(BF16), ((1,), (1,)))
    put_row = lax.broadcasted_iota(jnp.int32, (16, 128), 0)
    put_lane = lax.broadcasted_iota(jnp.int32, (16, 128), 1)
    spread = [[], []]
    for part in range(2):
        total_hi = jnp.zeros((table.shape[0], 128), F32)
        total_lo = jnp.zeros((table.shape[0], 128), F32)
        for row in range(rows):
            put = jnp.where(put_row + 16 * row == put_lane, 1.0, 0.0).astype(BF16)
            high, low = halves(table[:, row, part, :])
            total_hi = total_hi + dot(high, put, ((1,), (0,)))
            total_lo = total_lo + dot(low, put, ((1,), (0,)))
        spread[0].append(total_hi.astype(BF16))
        spread[1].append(total_lo.astype(BF16))
    t_hi = jnp.concatenate(spread[0], axis=1)
    t_lo = jnp.concatenate(spread[1], axis=1)
    lane_f = lane.astype(F32)
    kind_f = lax.broadcasted_iota(jnp.int32, (clusters, table.shape[0]), 1).astype(F32)
    for link in range(far_count):
        picks[link] = jnp.where(wanted[:, link : link + 1] == lane_f, 1.0, 0.0).astype(BF16)
        chosen = jnp.where(kinds[:, link : link + 1] == kind_f, 1.0, 0.0).astype(BF16)
        operators[link] = dot(chosen, t_hi, ((1,), (0,))) + dot(chosen, t_lo, ((1,), (0,)))

    for copy in halos:
        copy.wait()

    for row in range(rows):
        total = jnp.zeros((64, columns), F32)
        for step in range(9):
            part = (below, child, above)[step // 3][step % 3]
            total = total + theta[row, step] * part
        high, low = halves(total)
        lhs_hi[row * 64 : (row + 1) * 64, :] = high
        lhs_lo[row * 64 : (row + 1) * 64, :] = low

    plane = lax.div(me, 16)
    seat = lax.rem(me, 16)
    half_w = lax.broadcasted_iota(jnp.int32, (8, 256), 0) < 4
    for turn in (2, 1, 3, 0):
        block = lax.rem(plane + turn, 4)
        lanes = pl.ds(pl.multiple_of(block * 256, 256), 256)
        refined = dot3(lhs_hi[...], lhs_lo[...], phi_hi[:, lanes], phi_lo[:, lanes], ((1,), (0,)))
        fields = []
        for row in range(rows):
            straight = jnp.zeros((8, 256), F32)
            crossed = jnp.zeros((8, 256), F32)
            for octant in range(8):
                piece = refined[row * 64 + octant * 8 : row * 64 + octant * 8 + 8]
                straight = straight + piece * cosine[0, row, octant : octant + 1, lanes]
                crossed = crossed + piece * sine[0, row, octant : octant + 1, lanes]
            crossed = pltpu.roll(crossed, 4, 0)
            field = straight + jnp.where(half_w, -crossed, crossed)
            fields += [field[:, :128], field[:, 128:]]
        packed = swap_groups(jnp.stack(fields, axis=0))
        for row in range(rows):
            for side in range(2):
                msg_out[pl.ds(block * 16 + side * 8, 8), row, :] = packed[row * 2 + side]

        def send(step, carry):
            target = block * 16 + lax.rem(seat + step, 16)
            pltpu.make_async_remote_copy(
                src_ref=msg_out.at[target], dst_ref=msg_in.at[me], send_sem=a2a_send, recv_sem=a2a_recv,
                device_id=(target, ring), device_id_type=MESH,
            ).start()
            return carry

        if turn == 0:
            lax.fori_loop(1, 16, send, 0)
        else:
            lax.fori_loop(4, 20, send, 0)

    own = pltpu.make_async_copy(msg_out.at[me], msg_in.at[me], own_sem.at[0])
    own.start()
    own.wait()
    pltpu.make_async_copy(msg_out.at[others], msg_in.at[others], a2a_recv).wait()

    group = lax.broadcasted_iota(jnp.int32, (n_clus, 128), 1) // 16
    arrived = [msg_in[:, row, :] for row in range(rows)]
    gathered = [[], []]
    for part in range(2):
        for place in range(inner):
            total = jnp.zeros((n_clus, 128), F32)
            for row in range(rows):
                shift = 16 * (row - part * inner - place)
                total = jnp.where(group == row, pltpu.roll(arrived[row], shift % 128, 1), total)
            gathered[part].append(total)
    x_hi, x_lo = halves(
        jnp.concatenate([jnp.concatenate(gathered[0], axis=0), jnp.concatenate(gathered[1], axis=0)], axis=1)
    )
    in_re = jnp.zeros((clusters, 128), F32)
    in_im = jnp.zeros((clusters, 128), F32)
    for link in range(far_count):
        pick = picks[link]
        source = dot(pick, x_hi, ((1,), (0,))) + dot(pick, x_lo, ((1,), (0,)))
        s_re, s_im = source[:, :128], source[:, 128:]
        o_re, o_im = operators[link, :, :128], operators[link, :, 128:]
        in_re = in_re + (o_re * s_re - o_im * s_im)
        in_im = in_im + (o_re * s_im + o_im * s_re)
    for row in range(rows):
        total = jnp.zeros((n_clus, 128), F32)
        for part, field in enumerate((in_re, in_im)):
            for place in range(inner):
                spot_of = part * inner + place
                piece = field[place * n_clus : (place + 1) * n_clus]
                total = jnp.where(group == spot_of, pltpu.roll(piece, (16 * (spot_of - row)) % 128, 1), total)
        back_out[:, row, :] = total

    def give(step, carry):
        target = lax.rem(me + step, n_clus)
        pltpu.make_async_remote_copy(
            src_ref=back_out.at[target], dst_ref=back_in.at[me], send_sem=back_send, recv_sem=back_recv,
            device_id=(target, ring), device_id_type=MESH,
        ).start()
        return carry

    lax.fori_loop(1, n_clus, give, 0)
    own = pltpu.make_async_copy(back_out.at[me], back_in.at[me], own_sem.at[1])
    own.start()

    for copy in tilts:
        copy.wait()
    for place in (1, 2):
        for row in range(rows):
            angle = cosine[place, row]
            sine[place, row] = jnp.sin(angle)
            cosine[place, row] = jnp.cos(angle)

    own.wait()
    pltpu.make_async_copy(back_out.at[others], back_in.at[others], back_recv).wait()

    for row in range(rows):
        field = swap_groups(back_in[:, row, :].reshape(n_clus // 8, 8, 128))
        for block in range(n_clus // 8):
            inc_out[row, :, block * 128 : (block + 1) * 128] = field[block]
    passes = [
        pltpu.make_async_remote_copy(
            src_ref=inc_out, dst_ref=target, send_sem=inc_send.at[place], recv_sem=inc_recv.at[place],
            device_id=(me, side), device_id_type=MESH,
        )
        for place, (target, side) in enumerate([(inc_far, away), (inc_pair, pair)])
    ]
    for copy in passes:
        copy.start()

    half = lax.broadcasted_iota(jnp.int32, (8, 128), 0) < 4

    def lower(source, place, base):
        for block in range(azimuth // 128):
            lanes = slice(block * 128, (block + 1) * 128)
            straight = [source[row, :, lanes] for row in range(rows)]
            crossed = []
            for row in range(rows):
                swapped = pltpu.roll(straight[row], 4, 0)
                crossed.append(jnp.where(half, swapped, -swapped))
            scale = [[theta[row, base + step] for step in range(3)] for row in range(rows)]
            for octant in range(0, 8, 2):
                sums = [[], [], []]
                for one in (octant, octant + 1):
                    totals = [jnp.zeros((8, 128), F32)] * 3
                    for row in range(rows):
                        piece = (
                            straight[row] * cosine[place, row, one : one + 1, lanes]
                            + crossed[row] * sine[place, row, one : one + 1, lanes]
                        )
                        totals = [total + scale[row][step] * piece for step, total in enumerate(totals)]
                    for step in range(3):
                        sums[step].append(totals[step])
                for step in range(3):
                    span = slice(step * 64 + octant * 8, step * 64 + octant * 8 + 16)
                    value = jnp.concatenate(sums[step], axis=0)
                    if place > 0:
                        value = value + total_low[span, lanes]
                    if place < 2:
                        total_low[span, lanes] = value
                    else:
                        high, low = halves(value)
                        low_hi[span, lanes] = high
                        low_lo[span, lanes] = low

    lower(inc_out, 0, 3)
    passes[1].wait()
    lower(inc_pair, 1, 6 * core)
    pltpu.make_async_copy(msg_out.at[others], msg_in.at[others], a2a_send).wait()
    pltpu.make_async_copy(back_out.at[others], back_in.at[others], back_send).wait()
    passes[0].wait()
    lower(inc_far, 2, 6 - 6 * core)

    for cut in range(0, columns, 256):
        span = slice(cut, cut + 256)
        narrow = dot3(low_hi[...], low_lo[...], phi_hi[span, :], phi_lo[span, :], ((1,), (1,)))
        for step in range(3):
            child_out[step, :, span] = narrow[step * 64 : (step + 1) * 64]


def per_device(n_clus, n_samp, child_patterns, theta_weights, phi_stencil, phi_weights, shift_phase, translation_table, far_list, far_vector):
    groups = child_patterns.shape[0] // 8
    own_rows, columns = child_patterns.shape[2:]
    rows = theta_weights.shape[0]
    azimuth = phi_stencil.shape[0]
    clusters, far_count = far_list.shape
    child = child_patterns.reshape(groups, 8, 2, own_rows, columns).transpose(3, 1, 2, 0, 4)
    child = child.reshape(own_rows, groups * 16, columns)
    vmem = pl.BlockSpec(memory_space=pltpu.VMEM)
    smem = pl.BlockSpec(memory_space=pltpu.SMEM)
    hbm = pl.BlockSpec(memory_space=pltpu.HBM)
    block = (own_rows, groups * 16, columns)
    field = (rows, 8, azimuth)
    stencil, weights = phi_stencil.T, phi_weights.T
    phase = shift_phase.transpose(1, 0, 2)
    table = translation_table.transpose(0, 2, 1, 3)
    far, vec = far_list.T, far_vector.T
    mail = pltpu.VMEM((n_clus, rows, 128), F32)
    incoming, child_incoming = pl.pallas_call(
        functools.partial(window, n_clus, n_samp),
        out_shape=(jax.ShapeDtypeStruct(field, F32), jax.ShapeDtypeStruct(block, F32)),
        in_specs=[smem, vmem] + [hbm] * 6,
        out_specs=(vmem, vmem),
        scratch_shapes=[
            pltpu.VMEM(stencil.shape, jnp.int32),
            pltpu.VMEM(weights.shape, F32),
            pltpu.VMEM(field, F32),
            pltpu.VMEM(table.shape, F32),
            pltpu.VMEM(far.shape, jnp.int32),
            pltpu.VMEM(vec.shape, jnp.int32),
            pltpu.VMEM((columns, azimuth), BF16),
            pltpu.VMEM((columns, azimuth), BF16),
            pltpu.VMEM((3,) + field, F32),
            pltpu.VMEM((3,) + field, F32),
            pltpu.VMEM((far_count, clusters, clusters), BF16),
            pltpu.VMEM((far_count, clusters, 256), F32),
            pltpu.VMEM(block, F32),
            pltpu.VMEM(block, F32),
            pltpu.VMEM((rows * 64, columns), BF16),
            pltpu.VMEM((rows * 64, columns), BF16),
            pltpu.VMEM((own_rows * 64, azimuth), BF16),
            pltpu.VMEM((own_rows * 64, azimuth), BF16),
            pltpu.VMEM((own_rows * 64, azimuth), F32),
            mail,
            mail,
            mail,
            mail,
            pltpu.VMEM(field, F32),
            pltpu.VMEM(field, F32),
            pltpu.SemaphoreType.DMA((6,)),
            pltpu.SemaphoreType.DMA((2,)),
            pltpu.SemaphoreType.DMA((2,)),
            pltpu.SemaphoreType.DMA((2,)),
            pltpu.SemaphoreType.DMA((2,)),
            pltpu.SemaphoreType.DMA,
            pltpu.SemaphoreType.DMA,
            pltpu.SemaphoreType.DMA((2,)),
            pltpu.SemaphoreType.DMA,
            pltpu.SemaphoreType.DMA,
            pltpu.SemaphoreType.DMA((2,)),
            pltpu.SemaphoreType.DMA((2,)),
        ],
        compiler_params=pltpu.CompilerParams(collective_id=0, has_side_effects=True, vmem_limit_bytes=48 << 20),
    )(theta_weights, child, stencil, weights, phase, table, far, vec)
    incoming = incoming.reshape(rows, 2, groups, azimuth).transpose(2, 1, 0, 3)
    child_incoming = child_incoming.reshape(own_rows, 8, 2, groups, columns).transpose(3, 1, 2, 0, 4)
    return incoming, child_incoming.reshape(child_patterns.shape)


def solution(mesh):
    placed = (
        P("clus", None, "samp", None),
        P(),
        P(),
        P(),
        P(None, "samp", None),
        P(None, None, "samp", "clus"),
        P(),
        P(),
    )
    return jax.shard_map(
        functools.partial(per_device, mesh.shape["clus"], mesh.shape["samp"]),
        mesh=mesh,
        in_specs=placed,
        out_specs=(P("clus", None, "samp", None), P("clus", None, "samp", None)),
        check_vma=False,
    )
```

time: 85.4 us -> 73.7 us (0.86)
  the two profiles are of different devices: /device:TPU:6 before, /device:TPU:1 now
where the time goes in v3:
time: 73.7 us; the launch traced here: 73.2 us
  Pallas kernels  68.3 us (93%)
  local copies, waits for them, and re-layouts  4.14 us (6%)
    pallas_call x1, Pallas kernels, per_device(): pl.pallas_call(functools.partial(window, n_clus, n_samp), out_shape=(jax....  68.3 us

profile of v3, /device:TPU:1, one launch (start us, length us, event | category | flops | bytes accessed | tf_op | source)
XLA Modules:
  0.0 73.2 jit_solution(9283506655379168091)
XLA Ops:
  0.6 1.3 %copy.15 = f32[4,8,2,3,512]{4,0,2,1,3:T(4,128)S(1)} copy(f32[4,8,2,3,512]{4,2,3,1,0:T(2,128)} %bitcast.23) | data formatting | bytes 786432 | tf_op jit(solution)/shard_map/reshape | solution.py:335
  1.9 0.0 copy-start
  1.9 0.0 copy-start.1
  1.9 0.0 copy-start.2
  1.9 0.0 copy-start.3
  1.9 0.0 copy-start.4
  1.9 0.0 copy-start.5
  2.0 0.0 copy-start.6
  2.0 0.1 reshape.20.child
  2.1 0.7 copy-done
  2.8 0.1 copy-done.1
  2.9 0.0 copy-done.2
  2.9 0.0 copy-done.3
  2.9 0.0 copy-done.4
  2.9 0.0 copy-done.5
  2.9 0.0 copy-done.6
  2.9 68.3 %shard_map.95 = (f32[6,8,1024]{2,1,0:T(8,128)S(1)}, f32[3,64,512]{2,1,0:T(8,128)S(1)}) custom-call(f32[6,9]{1,0:T(8,128)S(1)} %copy-done.6, f32[3,64,512]{2,1,0:T(8,128)S(1)} %reshape.20.child, s32[6,1024]{1,0:T(8,128)S(1)} %bitcast.17, f32[6,1024]{1,0:T(8,128)S(1)} %bitcast.18, f32[6,8,1024]{2,1,0:T(8,128)S(1)} %bitcast.15, f32[16,6,2,16]{3,2,1,0:T(2,128)S(1)} %bitcast.16, ...), custom_call_target="tpu_custom_call" | custom-call | tf_op jit(solution)/shard_map/pallas_call | solution.py:347
  71.2 0.1 reshape.21
  71.3 0.8 %copy.16 = f32[6,2,4,1024]{3,1,0,2:T(2,128)} copy(f32[6,2,4,1024]{3,2,1,0:T(4,128)S(1)} %reshape.21) | data formatting | bytes 393216 | tf_op jit(solution)/shard_map/reshape | solution.py:393
  72.1 0.1 reshape.22
  72.2 0.9 %copy.12 = f32[4,8,2,3,512]{4,2,3,1,0:T(2,128)} copy(f32[4,8,2,3,512]{4,0,2,1,3:T(4,128)S(1)} %bitcast.21) | data formatting | bytes 786432 | tf_op jit(solution)/shard_map/transpose | solution.py:394
Async XLA Ops:
  1.9 0.9 %copy-start = (f32[8,6,1024]{2,0,1:T(8,128)S(1)}, f32[8,6,1024]{2,0,1:T(8,128)}, u32[]{:S(2)}) copy-start(f32[8,6,1024]{2,0,1:T(8,128)} %param.12) | copy-start | bytes 589828
  1.9 1.0 %copy-start.1 = (f32[16,2,6,16]{3,1,2,0:T(2,128)S(1)}, f32[16,2,6,16]{3,1,2,0:T(2,128)}, u32[]{:S(2)}) copy-start(f32[16,2,6,16]{3,1,2,0:T(2,128)} %param.13) | copy-start | bytes 36868
  1.9 1.0 %copy-start.2 = (s32[1024,6]{0,1:T(8,128)S(1)}, s32[1024,6]{0,1:T(8,128)}, u32[]{:S(2)}) copy-start(s32[1024,6]{0,1:T(8,128)} %param.10) | copy-start | bytes 73732
  1.9 1.0 %copy-start.3 = (f32[1024,6]{0,1:T(8,128)S(1)}, f32[1024,6]{0,1:T(8,128)}, u32[]{:S(2)}) copy-start(f32[1024,6]{0,1:T(8,128)} %param.11) | copy-start | bytes 73732
  1.9 1.0 %copy-start.4 = (s32[256,12]{0,1:T(8,128)S(1)}, s32[256,12]{0,1:T(8,128)}, u32[]{:S(2)}) copy-start(s32[256,12]{0,1:T(8,128)} %param.14) | copy-start | bytes 36868
  1.9 0.9 %copy-start.5 = (s32[256,12]{0,1:T(8,128)S(1)}, s32[256,12]{0,1:T(8,128)}, u32[]{:S(2)}) copy-start(s32[256,12]{0,1:T(8,128)} %param.15) | copy-start | bytes 36868
  2.0 0.9 %copy-start.6 = (f32[6,9]{1,0:T(8,128)S(1)}, f32[6,9]{1,0:T(8,128)}, u32[]{:S(2)}) copy-start(f32[6,9]{1,0:T(8,128)} %theta.1) | copy-start | bytes 652

commit v4 on v3

--- a/solution.py
+++ b/solution.py
@@ -45,7 +45,7 @@
     below, above, lhs_hi, lhs_lo, low_hi, low_lo, total_low,
     msg_out, msg_in, back_out, back_in, inc_pair, inc_far,
     in_sem, halo_send, halo_recv, phase_send, phase_recv,
-    a2a_send, a2a_recv, own_sem, back_send, back_recv, inc_send, inc_recv,
+    a2a_send, a2a_recv, own_sem, back_send, back_recv, inc_send, inc_recv, zone,
 ):
     me = lax.axis_index("clus")
     ring = lax.axis_index("samp")
@@ -70,38 +70,28 @@
             [(stencil_in, stencil), (weights_in, weights), (phase_in, phase), (table_in, table), (far_in, far), (vec_in, vec)]
         )
     ]
+    barrier = pltpu.get_barrier_semaphore()
+    layers = [(me + 4 * (lax.rem(deep + by, 4) - deep), ring) for by in (1, 3)]
+    for peer in [(me, up), (me, down), (near, away)] + layers:
+        pl.semaphore_signal(barrier, inc=1, device_id=peer, device_id_type=MESH)
+    plane = lax.div(me, 16)
+    across = lax.rem(me, 4)
+
+    def greet(step, carry):
+        peer = lax.rem(plane + lax.div(step, 4), 4) * 16 + deep * 4 + lax.rem(across + lax.rem(step, 4), 4)
+        pl.semaphore_signal(barrier, inc=1, device_id=(peer, ring), device_id_type=MESH)
+        return carry
+
+    lax.fori_loop(1, 16, greet, 0)
     for copy in loads:
         copy.start()
 
-    barrier = pltpu.get_barrier_semaphore()
-    for peer in ((me, up), (me, down), (near, away)):
-        pl.semaphore_signal(barrier, inc=1, device_id=peer, device_id_type=MESH)
-
-    def greet(step, carry):
-        pl.semaphore_signal(barrier, inc=1, device_id=(lax.rem(me + step, n_clus), ring), device_id_type=MESH)
-        return carry
-
-    lax.fori_loop(1, n_clus, greet, 0)
-
-    loads[0].wait()
-    loads[1].wait()
-
-    def build(step, carry):
-        first = pl.multiple_of(step * 32, 32)
-        places = lax.broadcasted_iota(jnp.int32, (32, azimuth), 0) + first
-        total = jnp.zeros((32, azimuth), F32)
-        for point in range(stencil.shape[0]):
-            total = total + jnp.where(stencil[point : point + 1, :] == places, weights[point : point + 1, :], 0.0)
-        high, low = halves(total)
-        phi_hi[pl.ds(first, 32), :] = high
-        phi_lo[pl.ds(first, 32), :] = low
-        return carry
-
-    lax.fori_loop(0, columns // 32, build, 0)
-    for copy in loads[2:]:
-        copy.wait()
-
-    pl.semaphore_wait(barrier, n_clus + 2)
+    def tell(stage):
+        for peer in layers:
+            pl.semaphore_signal(zone.at[stage], inc=1, device_id=peer, device_id_type=MESH)
+
+    loads[2].wait()
+    pl.semaphore_wait(barrier, 20)
     halos = [
         pltpu.make_async_remote_copy(
             src_ref=child, dst_ref=target, send_sem=halo_send.at[place], recv_sem=halo_recv.at[place],
@@ -120,15 +110,37 @@
     ]
     for copy in tilts:
         copy.start()
+    tell(0)
 
     for row in range(rows):
         cosine[0, row] = jnp.cos(phase[row])
         sine[0, row] = jnp.sin(phase[row])
 
+    pl.semaphore_wait(zone.at[0], 2)
+    tell(1)
+    loads[0].wait()
+    loads[1].wait()
+
+    def build(step, carry):
+        first = pl.multiple_of(step * 32, 32)
+        places = lax.broadcasted_iota(jnp.int32, (32, azimuth), 0) + first
+        total = jnp.zeros((32, azimuth), F32)
+        for point in range(stencil.shape[0]):
+            total = total + jnp.where(stencil[point : point + 1, :] == places, weights[point : point + 1, :], 0.0)
+        high, low = halves(total)
+        phi_hi[pl.ds(first, 32), :] = high
+        phi_lo[pl.ds(first, 32), :] = low
+        return carry
+
+    lax.fori_loop(0, columns // 32, build, 0)
+    for copy in loads[3:]:
+        copy.wait()
+
     inner = clusters // n_clus
     spot = lax.broadcasted_iota(jnp.int32, (clusters, clusters), 0)
     lane = lax.broadcasted_iota(jnp.int32, (clusters, clusters), 1)
-    order = jnp.where((spot % n_clus) * inner + spot // n_clus == lane, 1.0, 0.0).astype(BF16)
+    named = ((spot // 64) * 16 + spot % 16) * inner + (spot // 16) % inner
+    order = jnp.where(named == lane, 1.0, 0.0).astype(BF16)
     partner = far[...]
     partner = (partner % inner) * n_clus + partner // inner
     wanted = dot(order, partner.astype(F32).astype(BF16), ((1,), (1,)))
@@ -151,9 +163,12 @@
     lane_f = lane.astype(F32)
     kind_f = lax.broadcasted_iota(jnp.int32, (clusters, table.shape[0]), 1).astype(F32)
     for link in range(far_count):
-        picks[link] = jnp.where(wanted[:, link : link + 1] == lane_f, 1.0, 0.0).astype(BF16)
+        pick = jnp.where(wanted[:, link : link + 1] == lane_f, 1.0, 0.0).astype(BF16)
         chosen = jnp.where(kinds[:, link : link + 1] == kind_f, 1.0, 0.0).astype(BF16)
-        operators[link] = dot(chosen, t_hi, ((1,), (0,))) + dot(chosen, t_lo, ((1,), (0,)))
+        operator = dot(chosen, t_hi, ((1,), (0,))) + dot(chosen, t_lo, ((1,), (0,)))
+        for part in range(4):
+            picks[part, link * 64 : (link + 1) * 64, :] = pick[part * 64 : (part + 1) * 64]
+            operators[part, link * 64 : (link + 1) * 64, :] = operator[part * 64 : (part + 1) * 64]
 
     for copy in halos:
         copy.wait()
@@ -167,13 +182,39 @@
         lhs_hi[row * 64 : (row + 1) * 64, :] = high
         lhs_lo[row * 64 : (row + 1) * 64, :] = low
 
-    plane = lax.div(me, 16)
+    pl.semaphore_wait(zone.at[1], 2)
     seat = lax.rem(me, 16)
     half_w = lax.broadcasted_iota(jnp.int32, (8, 256), 0) < 4
-    for turn in (2, 1, 3, 0):
+    turns = (2, 1, 3, 0)
+
+    def mail_plane(turn, outbox, inbox, send_sem, recv_sem):
         block = lax.rem(plane + turn, 4)
-        lanes = pl.ds(pl.multiple_of(block * 256, 256), 256)
-        refined = dot3(lhs_hi[...], lhs_lo[...], phi_hi[:, lanes], phi_lo[:, lanes], ((1,), (0,)))
+
+        def send(step, carry):
+            target = block * 16 + lax.rem(seat + step, 16)
+            pltpu.make_async_remote_copy(
+                src_ref=outbox.at[target], dst_ref=inbox.at[me], send_sem=send_sem, recv_sem=recv_sem,
+                device_id=(target, ring), device_id_type=MESH,
+            ).start()
+            return carry
+
+        if turn == 0:
+            lax.fori_loop(1, 16, send, 0)
+        else:
+            lax.fori_loop(4, 20, send, 0)
+
+    def spans(turn):
+        return pl.ds(pl.multiple_of(lax.rem(plane + turn, 4) * 256, 256), 256)
+
+    def refine(turn):
+        lanes = spans(turn)
+        return dot3(lhs_hi[...], lhs_lo[...], phi_hi[:, lanes], phi_lo[:, lanes], ((1,), (0,)))
+
+    refined = refine(turns[0])
+    for place, turn in enumerate(turns):
+        block = lax.rem(plane + turn, 4)
+        lanes = spans(turn)
+        following = refine(turns[place + 1]) if place < 3 else None
         fields = []
         for row in range(rows):
             straight = jnp.zeros((8, 256), F32)
@@ -189,19 +230,8 @@
         for row in range(rows):
             for side in range(2):
                 msg_out[pl.ds(block * 16 + side * 8, 8), row, :] = packed[row * 2 + side]
-
-        def send(step, carry):
-            target = block * 16 + lax.rem(seat + step, 16)
-            pltpu.make_async_remote_copy(
-                src_ref=msg_out.at[target], dst_ref=msg_in.at[me], send_sem=a2a_send, recv_sem=a2a_recv,
-                device_id=(target, ring), device_id_type=MESH,
-            ).start()
-            return carry
-
-        if turn == 0:
-            lax.fori_loop(1, 16, send, 0)
-        else:
-            lax.fori_loop(4, 20, send, 0)
+        mail_plane(turn, msg_out, msg_in, a2a_send, a2a_recv)
+        refined = following
 
     own = pltpu.make_async_copy(msg_out.at[me], msg_in.at[me], own_sem.at[0])
     own.start()
@@ -221,33 +251,35 @@
     x_hi, x_lo = halves(
         jnp.concatenate([jnp.concatenate(gathered[0], axis=0), jnp.concatenate(gathered[1], axis=0)], axis=1)
     )
-    in_re = jnp.zeros((clusters, 128), F32)
-    in_im = jnp.zeros((clusters, 128), F32)
-    for link in range(far_count):
-        pick = picks[link]
-        source = dot(pick, x_hi, ((1,), (0,))) + dot(pick, x_lo, ((1,), (0,)))
-        s_re, s_im = source[:, :128], source[:, 128:]
-        o_re, o_im = operators[link, :, :128], operators[link, :, 128:]
-        in_re = in_re + (o_re * s_re - o_im * s_im)
-        in_im = in_im + (o_re * s_im + o_im * s_re)
-    for row in range(rows):
-        total = jnp.zeros((n_clus, 128), F32)
-        for part, field in enumerate((in_re, in_im)):
-            for place in range(inner):
-                spot_of = part * inner + place
-                piece = field[place * n_clus : (place + 1) * n_clus]
-                total = jnp.where(group == spot_of, pltpu.roll(piece, (16 * (spot_of - row)) % 128, 1), total)
-        back_out[:, row, :] = total
-
-    def give(step, carry):
-        target = lax.rem(me + step, n_clus)
-        pltpu.make_async_remote_copy(
-            src_ref=back_out.at[target], dst_ref=back_in.at[me], send_sem=back_send, recv_sem=back_recv,
-            device_id=(target, ring), device_id_type=MESH,
-        ).start()
-        return carry
-
-    lax.fori_loop(1, n_clus, give, 0)
+    group = lax.broadcasted_iota(jnp.int32, (16, 128), 1) // 16
+
+    def fetch(turn):
+        pick = picks[lax.rem(plane + turn, 4)]
+        return dot(pick, x_hi, ((1,), (0,))) + dot(pick, x_lo, ((1,), (0,)))
+
+    source = fetch(turns[0])
+    for place, turn in enumerate(turns):
+        block = lax.rem(plane + turn, 4)
+        following = fetch(turns[place + 1]) if place < 3 else None
+        in_re = jnp.zeros((64, 128), F32)
+        in_im = jnp.zeros((64, 128), F32)
+        for link in range(far_count):
+            span = slice(link * 64, (link + 1) * 64)
+            s_re, s_im = source[span, :128], source[span, 128:]
+            o_re, o_im = operators[block, span, :128], operators[block, span, 128:]
+            in_re = in_re + (o_re * s_re - o_im * s_im)
+            in_im = in_im + (o_re * s_im + o_im * s_re)
+        for row in range(rows):
+            total = jnp.zeros((16, 128), F32)
+            for part, field in enumerate((in_re, in_im)):
+                for seat_in in range(inner):
+                    spot_of = part * inner + seat_in
+                    piece = field[seat_in * 16 : (seat_in + 1) * 16]
+                    total = jnp.where(group == spot_of, pltpu.roll(piece, (16 * (spot_of - row)) % 128, 1), total)
+            back_out[pl.ds(block * 16, 16), row, :] = total
+        mail_plane(turn, back_out, back_in, back_send, back_recv)
+        source = following
+
     own = pltpu.make_async_copy(back_out.at[me], back_in.at[me], own_sem.at[1])
     own.start()
 
@@ -266,20 +298,27 @@
         field = swap_groups(back_in[:, row, :].reshape(n_clus // 8, 8, 128))
         for block in range(n_clus // 8):
             inc_out[row, :, block * 128 : (block + 1) * 128] = field[block]
+    wide = azimuth // 2
     passes = [
         pltpu.make_async_remote_copy(
-            src_ref=inc_out, dst_ref=target, send_sem=inc_send.at[place], recv_sem=inc_recv.at[place],
+            src_ref=origin, dst_ref=target, send_sem=inc_send.at[place], recv_sem=inc_recv.at[place],
             device_id=(me, side), device_id_type=MESH,
         )
-        for place, (target, side) in enumerate([(inc_far, away), (inc_pair, pair)])
+        for place, (origin, target, side) in enumerate(
+            [
+                (inc_out.at[:, :, pl.ds(0, wide)], inc_far.at[:, :, pl.ds(0, wide)], away),
+                (inc_out.at[:, :, pl.ds(wide, wide)], inc_far.at[:, :, pl.ds(wide, wide)], away),
+                (inc_out, inc_pair, pair),
+            ]
+        )
     ]
     for copy in passes:
         copy.start()
 
     half = lax.broadcasted_iota(jnp.int32, (8, 128), 0) < 4
 
-    def lower(source, place, base):
-        for block in range(azimuth // 128):
+    def lower(source, place, base, blocks):
+        for block in blocks:
             lanes = slice(block * 128, (block + 1) * 128)
             straight = [source[row, :, lanes] for row in range(rows)]
             crossed = []
@@ -311,19 +350,22 @@
                         low_hi[span, lanes] = high
                         low_lo[span, lanes] = low
 
-    lower(inc_out, 0, 3)
-    passes[1].wait()
-    lower(inc_pair, 1, 6 * core)
+    blocks = azimuth // 128
+    lower(inc_out, 0, 3, range(blocks))
+    passes[2].wait()
+    lower(inc_pair, 1, 6 * core, range(blocks))
     pltpu.make_async_copy(msg_out.at[others], msg_in.at[others], a2a_send).wait()
     pltpu.make_async_copy(back_out.at[others], back_in.at[others], back_send).wait()
-    passes[0].wait()
-    lower(inc_far, 2, 6 - 6 * core)
-
-    for cut in range(0, columns, 256):
-        span = slice(cut, cut + 256)
-        narrow = dot3(low_hi[...], low_lo[...], phi_hi[span, :], phi_lo[span, :], ((1,), (1,)))
-        for step in range(3):
-            child_out[step, :, span] = narrow[step * 64 : (step + 1) * 64]
+    for part in range(2):
+        passes[part].wait()
+        lower(inc_far, 2, 6 - 6 * core, range(part * blocks // 2, (part + 1) * blocks // 2))
+        lanes = slice(part * wide, (part + 1) * wide)
+        for cut in range(0, columns, 256):
+            span = slice(cut, cut + 256)
+            narrow = dot3(low_hi[:, lanes], low_lo[:, lanes], phi_hi[span, lanes], phi_lo[span, lanes], ((1,), (1,)))
+            for step in range(3):
+                value = narrow[step * 64 : (step + 1) * 64]
+                child_out[step, :, span] = value if part == 0 else child_out[step, :, span] + value
 
 
 def per_device(n_clus, n_samp, child_patterns, theta_weights, phi_stencil, phi_weights, shift_phase, translation_table, far_list, far_vector):
@@ -360,8 +402,8 @@
             pltpu.VMEM((columns, azimuth), BF16),
             pltpu.VMEM((3,) + field, F32),
             pltpu.VMEM((3,) + field, F32),
-            pltpu.VMEM((far_count, clusters, clusters), BF16),
-            pltpu.VMEM((far_count, clusters, 256), F32),
+            pltpu.VMEM((4, far_count * 64, clusters), BF16),
+            pltpu.VMEM((4, far_count * 64, 256), F32),
             pltpu.VMEM(block, F32),
             pltpu.VMEM(block, F32),
             pltpu.VMEM((rows * 64, columns), BF16),
@@ -385,8 +427,9 @@
             pltpu.SemaphoreType.DMA((2,)),
             pltpu.SemaphoreType.DMA,
             pltpu.SemaphoreType.DMA,
-            pltpu.SemaphoreType.DMA((2,)),
-            pltpu.SemaphoreType.DMA((2,)),
+            pltpu.SemaphoreType.DMA((3,)),
+            pltpu.SemaphoreType.DMA((3,)),
+            pltpu.SemaphoreType.REGULAR((2,)),
         ],
         compiler_params=pltpu.CompilerParams(collective_id=0, has_side_effects=True, vmem_limit_bytes=48 << 20),
     )(theta_weights, child, stencil, weights, phase, table, far, vec)

time: 73.7 us -> 67.9 us (0.921)
  Pallas kernels: 68.3 us -> 62.9 us
    pallas_call x1, Pallas kernels: 68.3 us -> 62.9 us  [per_device(): pl.pallas_call(functools.partial(window, n_clus, n_samp), out_shape=(jax....]
where the time goes in v4:
time: 67.9 us; the launch traced here: 67.7 us
  Pallas kernels  62.9 us (93%)
  local copies, waits for them, and re-layouts  4.14 us (6%)
  between operations  0.73 us (1%)
    pallas_call x1, Pallas kernels, per_device(): pl.pallas_call(functools.partial(window, n_clus, n_samp), out_shape=(jax....  62.9 us

profile of v4, /device:TPU:1, one launch (start us, length us, event | category | flops | bytes accessed | tf_op | source)
XLA Modules:
  0.0 67.7 jit_solution(16043986812667412481)
XLA Ops:
  0.6 1.3 %copy.15 = f32[4,8,2,3,512]{4,0,2,1,3:T(4,128)S(1)} copy(f32[4,8,2,3,512]{4,2,3,1,0:T(2,128)} %bitcast.23) | data formatting | bytes 786432 | tf_op jit(solution)/shard_map/reshape | solution.py:377
  1.9 0.0 copy-start
  1.9 0.0 copy-start.1
  1.9 0.0 copy-start.2
  1.9 0.0 copy-start.3
  1.9 0.0 copy-start.4
  1.9 0.0 copy-start.5
  2.0 0.0 copy-start.6
  2.0 0.1 reshape.20.child
  2.1 0.7 %copy-done = f32[8,6,1024]{2,0,1:T(8,128)S(1)} copy-done((f32[8,6,1024]{2,0,1:T(8,128)S(1)}, f32[8,6,1024]{2,0,1:T(8,128)}, u32[]{:S(2)}) %copy-start) | copy-done | bytes 196632
  2.8 0.1 copy-done.1
  2.9 0.0 copy-done.2
  2.9 0.0 copy-done.3
  2.9 0.0 copy-done.4
  2.9 0.0 copy-done.5
  2.9 0.0 copy-done.6
  2.9 62.9 %shard_map.95 = (f32[6,8,1024]{2,1,0:T(8,128)S(1)}, f32[3,64,512]{2,1,0:T(8,128)S(1)}) custom-call(f32[6,9]{1,0:T(8,128)S(1)} %copy-done.6, f32[3,64,512]{2,1,0:T(8,128)S(1)} %reshape.20.child, s32[6,1024]{1,0:T(8,128)S(1)} %bitcast.17, f32[6,1024]{1,0:T(8,128)S(1)} %bitcast.18, f32[6,8,1024]{2,1,0:T(8,128)S(1)} %bitcast.15, f32[16,6,2,16]{3,2,1,0:T(2,128)S(1)} %bitcast.16, ...), custom_call_target="tpu_custom_call" | custom-call | tf_op jit(solution)/shard_map/pallas_call | solution.py:389
  65.8 0.1 reshape.21
  65.8 0.8 %copy.16 = f32[6,2,4,1024]{3,1,0,2:T(2,128)} copy(f32[6,2,4,1024]{3,2,1,0:T(4,128)S(1)} %reshape.21) | data formatting | bytes 393216 | tf_op jit(solution)/shard_map/reshape | solution.py:436
  66.7 0.1 reshape.22
  66.8 0.9 %copy.12 = f32[4,8,2,3,512]{4,2,3,1,0:T(2,128)} copy(f32[4,8,2,3,512]{4,0,2,1,3:T(4,128)S(1)} %bitcast.21) | data formatting | bytes 786432 | tf_op jit(solution)/shard_map/transpose | solution.py:437
Async XLA Ops:
  1.9 0.9 %copy-start = (f32[8,6,1024]{2,0,1:T(8,128)S(1)}, f32[8,6,1024]{2,0,1:T(8,128)}, u32[]{:S(2)}) copy-start(f32[8,6,1024]{2,0,1:T(8,128)} %param.12) | copy-start | bytes 589828
  1.9 1.0 %copy-start.1 = (f32[16,2,6,16]{3,1,2,0:T(2,128)S(1)}, f32[16,2,6,16]{3,1,2,0:T(2,128)}, u32[]{:S(2)}) copy-start(f32[16,2,6,16]{3,1,2,0:T(2,128)} %param.13) | copy-start | bytes 36868
  1.9 1.0 %copy-start.2 = (s32[1024,6]{0,1:T(8,128)S(1)}, s32[1024,6]{0,1:T(8,128)}, u32[]{:S(2)}) copy-start(s32[1024,6]{0,1:T(8,128)} %param.10) | copy-start | bytes 73732
  1.9 1.0 %copy-start.3 = (f32[1024,6]{0,1:T(8,128)S(1)}, f32[1024,6]{0,1:T(8,128)}, u32[]{:S(2)}) copy-start(f32[1024,6]{0,1:T(8,128)} %param.11) | copy-start | bytes 73732
  1.9 1.0 %copy-start.4 = (s32[256,12]{0,1:T(8,128)S(1)}, s32[256,12]{0,1:T(8,128)}, u32[]{:S(2)}) copy-start(s32[256,12]{0,1:T(8,128)} %param.14) | copy-start | bytes 36868
  1.9 0.9 %copy-start.5 = (s32[256,12]{0,1:T(8,128)S(1)}, s32[256,12]{0,1:T(8,128)}, u32[]{:S(2)}) copy-start(s32[256,12]{0,1:T(8,128)} %param.15) | copy-start | bytes 36868
  2.0 0.9 %copy-start.6 = (f32[6,9]{1,0:T(8,128)S(1)}, f32[6,9]{1,0:T(8,128)}, u32[]{:S(2)}) copy-start(f32[6,9]{1,0:T(8,128)} %theta.1) | copy-start | bytes 652

commit v5 on v4

--- a/solution.py
+++ b/solution.py
@@ -61,6 +61,7 @@
     columns = child.shape[2]
     azimuth = stencil.shape[1]
     rows = phase.shape[0]
+    some = rows // 2
     far_count, clusters = far.shape
     others = pl.ds(0, n_clus - 1)
 
@@ -147,28 +148,28 @@
     kinds = dot(order, vec[...].astype(F32).astype(BF16), ((1,), (1,)))
     put_row = lax.broadcasted_iota(jnp.int32, (16, 128), 0)
     put_lane = lax.broadcasted_iota(jnp.int32, (16, 128), 1)
-    spread = [[], []]
-    for part in range(2):
+    tables = []
+    for side in range(2):
         total_hi = jnp.zeros((table.shape[0], 128), F32)
         total_lo = jnp.zeros((table.shape[0], 128), F32)
-        for row in range(rows):
-            put = jnp.where(put_row + 16 * row == put_lane, 1.0, 0.0).astype(BF16)
-            high, low = halves(table[:, row, part, :])
-            total_hi = total_hi + dot(high, put, ((1,), (0,)))
-            total_lo = total_lo + dot(low, put, ((1,), (0,)))
-        spread[0].append(total_hi.astype(BF16))
-        spread[1].append(total_lo.astype(BF16))
-    t_hi = jnp.concatenate(spread[0], axis=1)
-    t_lo = jnp.concatenate(spread[1], axis=1)
+        for row in range(some):
+            for part in range(2):
+                put = jnp.where(put_row + (64 * part + 16 * row) == put_lane, 1.0, 0.0).astype(BF16)
+                high, low = halves(table[:, side * some + row, part, :])
+                total_hi = total_hi + dot(high, put, ((1,), (0,)))
+                total_lo = total_lo + dot(low, put, ((1,), (0,)))
+        tables.append((total_hi.astype(BF16), total_lo.astype(BF16)))
     lane_f = lane.astype(F32)
     kind_f = lax.broadcasted_iota(jnp.int32, (clusters, table.shape[0]), 1).astype(F32)
     for link in range(far_count):
         pick = jnp.where(wanted[:, link : link + 1] == lane_f, 1.0, 0.0).astype(BF16)
         chosen = jnp.where(kinds[:, link : link + 1] == kind_f, 1.0, 0.0).astype(BF16)
-        operator = dot(chosen, t_hi, ((1,), (0,))) + dot(chosen, t_lo, ((1,), (0,)))
         for part in range(4):
             picks[part, link * 64 : (link + 1) * 64, :] = pick[part * 64 : (part + 1) * 64]
-            operators[part, link * 64 : (link + 1) * 64, :] = operator[part * 64 : (part + 1) * 64]
+        for side, (t_hi, t_lo) in enumerate(tables):
+            operator = dot(chosen, t_hi, ((1,), (0,))) + dot(chosen, t_lo, ((1,), (0,)))
+            for part in range(4):
+                operators[side, part, link * 64 : (link + 1) * 64, :] = operator[part * 64 : (part + 1) * 64]
 
     for copy in halos:
         copy.wait()
@@ -206,82 +207,87 @@
     def spans(turn):
         return pl.ds(pl.multiple_of(lax.rem(plane + turn, 4) * 256, 256), 256)
 
-    def refine(turn):
+    steps = [(side, turn) for side in range(2) for turn in turns]
+
+    def refine(side, turn):
         lanes = spans(turn)
-        return dot3(lhs_hi[...], lhs_lo[...], phi_hi[:, lanes], phi_lo[:, lanes], ((1,), (0,)))
-
-    refined = refine(turns[0])
-    for place, turn in enumerate(turns):
+        span = slice(side * some * 64, (side + 1) * some * 64)
+        return dot3(lhs_hi[span, :], lhs_lo[span, :], phi_hi[:, lanes], phi_lo[:, lanes], ((1,), (0,)))
+
+    refined = refine(*steps[0])
+    for place, (side, turn) in enumerate(steps):
         block = lax.rem(plane + turn, 4)
         lanes = spans(turn)
-        following = refine(turns[place + 1]) if place < 3 else None
+        following = refine(*steps[place + 1]) if place + 1 < len(steps) else None
         fields = []
-        for row in range(rows):
+        for row in range(some):
             straight = jnp.zeros((8, 256), F32)
             crossed = jnp.zeros((8, 256), F32)
             for octant in range(8):
                 piece = refined[row * 64 + octant * 8 : row * 64 + octant * 8 + 8]
-                straight = straight + piece * cosine[0, row, octant : octant + 1, lanes]
-                crossed = crossed + piece * sine[0, row, octant : octant + 1, lanes]
+                straight = straight + piece * cosine[0, side * some + row, octant : octant + 1, lanes]
+                crossed = crossed + piece * sine[0, side * some + row, octant : octant + 1, lanes]
             crossed = pltpu.roll(crossed, 4, 0)
             field = straight + jnp.where(half_w, -crossed, crossed)
             fields += [field[:, :128], field[:, 128:]]
         packed = swap_groups(jnp.stack(fields, axis=0))
-        for row in range(rows):
-            for side in range(2):
-                msg_out[pl.ds(block * 16 + side * 8, 8), row, :] = packed[row * 2 + side]
-        mail_plane(turn, msg_out, msg_in, a2a_send, a2a_recv)
+        for row in range(some):
+            for part in range(2):
+                msg_out[side, pl.ds(block * 16 + part * 8, 8), row, :] = packed[row * 2 + part]
+        mail_plane(turn, msg_out.at[side], msg_in.at[side], a2a_send.at[side], a2a_recv.at[side])
         refined = following
 
-    own = pltpu.make_async_copy(msg_out.at[me], msg_in.at[me], own_sem.at[0])
-    own.start()
-    own.wait()
-    pltpu.make_async_copy(msg_out.at[others], msg_in.at[others], a2a_recv).wait()
-
-    group = lax.broadcasted_iota(jnp.int32, (n_clus, 128), 1) // 16
-    arrived = [msg_in[:, row, :] for row in range(rows)]
-    gathered = [[], []]
-    for part in range(2):
-        for place in range(inner):
+    owns = []
+    for side in range(2):
+        own = pltpu.make_async_copy(msg_out.at[side, me], msg_in.at[side, me], own_sem.at[side])
+        own.start()
+        owns.append(own)
+    group = lax.broadcasted_iota(jnp.int32, (n_clus, 128), 1) // 16 % 4
+    small = lax.broadcasted_iota(jnp.int32, (16, 128), 1) // 16 % 4
+    real = lax.broadcasted_iota(jnp.int32, (64, 128), 1) < 64
+    for side in range(2):
+        owns[side].wait()
+        pltpu.make_async_copy(msg_out.at[side, others], msg_in.at[side, others], a2a_recv.at[side]).wait()
+        arrived = [msg_in[side, :, row, :] for row in range(some)]
+        gathered = []
+        for seat_in in range(inner):
             total = jnp.zeros((n_clus, 128), F32)
-            for row in range(rows):
-                shift = 16 * (row - part * inner - place)
-                total = jnp.where(group == row, pltpu.roll(arrived[row], shift % 128, 1), total)
-            gathered[part].append(total)
-    x_hi, x_lo = halves(
-        jnp.concatenate([jnp.concatenate(gathered[0], axis=0), jnp.concatenate(gathered[1], axis=0)], axis=1)
-    )
-    group = lax.broadcasted_iota(jnp.int32, (16, 128), 1) // 16
-
-    def fetch(turn):
-        pick = picks[lax.rem(plane + turn, 4)]
-        return dot(pick, x_hi, ((1,), (0,))) + dot(pick, x_lo, ((1,), (0,)))
-
-    source = fetch(turns[0])
-    for place, turn in enumerate(turns):
-        block = lax.rem(plane + turn, 4)
-        following = fetch(turns[place + 1]) if place < 3 else None
-        in_re = jnp.zeros((64, 128), F32)
-        in_im = jnp.zeros((64, 128), F32)
-        for link in range(far_count):
-            span = slice(link * 64, (link + 1) * 64)
-            s_re, s_im = source[span, :128], source[span, 128:]
-            o_re, o_im = operators[block, span, :128], operators[block, span, 128:]
-            in_re = in_re + (o_re * s_re - o_im * s_im)
-            in_im = in_im + (o_re * s_im + o_im * s_re)
-        for row in range(rows):
-            total = jnp.zeros((16, 128), F32)
-            for part, field in enumerate((in_re, in_im)):
+            for row in range(some):
+                total = jnp.where(group == row, pltpu.roll(arrived[row], (16 * (row - seat_in)) % 128, 1), total)
+            gathered.append(total)
+        x_hi, x_lo = halves(jnp.concatenate(gathered, axis=0))
+
+        def fetch(turn):
+            pick = picks[lax.rem(plane + turn, 4)]
+            return dot(pick, x_hi, ((1,), (0,))) + dot(pick, x_lo, ((1,), (0,)))
+
+        source = fetch(turns[0])
+        for place, turn in enumerate(turns):
+            block = lax.rem(plane + turn, 4)
+            following = fetch(turns[place + 1]) if place < 3 else None
+            alike = jnp.zeros((64, 128), F32)
+            mixed = jnp.zeros((64, 128), F32)
+            for link in range(far_count):
+                span = slice(link * 64, (link + 1) * 64)
+                piece = source[span]
+                operator = operators[side, block, span, :]
+                alike = alike + operator * piece
+                mixed = mixed + operator * pltpu.roll(piece, 64, 1)
+            field = jnp.where(real, alike - pltpu.roll(alike, 64, 1), mixed + pltpu.roll(mixed, 64, 1))
+            for row in range(some):
+                total = jnp.zeros((16, 128), F32)
                 for seat_in in range(inner):
-                    spot_of = part * inner + seat_in
                     piece = field[seat_in * 16 : (seat_in + 1) * 16]
-                    total = jnp.where(group == spot_of, pltpu.roll(piece, (16 * (spot_of - row)) % 128, 1), total)
-            back_out[pl.ds(block * 16, 16), row, :] = total
-        mail_plane(turn, back_out, back_in, back_send, back_recv)
-        source = following
-
-    own = pltpu.make_async_copy(back_out.at[me], back_in.at[me], own_sem.at[1])
-    own.start()
+                    total = jnp.where(small == seat_in, pltpu.roll(piece, (16 * (seat_in - row)) % 128, 1), total)
+                back_out[side, pl.ds(block * 16, 16), row, :] = total
+            mail_plane(turn, back_out.at[side], back_in.at[side], back_send.at[side], back_recv.at[side])
+            source = following
+
+    owns = []
+    for side in range(2):
+        own = pltpu.make_async_copy(back_out.at[side, me], back_in.at[side, me], own_sem.at[2 + side])
+        own.start()
+        owns.append(own)
 
     for copy in tilts:
         copy.wait()
@@ -291,59 +297,37 @@
             sine[place, row] = jnp.sin(angle)
             cosine[place, row] = jnp.cos(angle)
 
-    own.wait()
-    pltpu.make_async_copy(back_out.at[others], back_in.at[others], back_recv).wait()
-
-    for row in range(rows):
-        field = swap_groups(back_in[:, row, :].reshape(n_clus // 8, 8, 128))
-        for block in range(n_clus // 8):
-            inc_out[row, :, block * 128 : (block + 1) * 128] = field[block]
-    wide = azimuth // 2
-    passes = [
-        pltpu.make_async_remote_copy(
-            src_ref=origin, dst_ref=target, send_sem=inc_send.at[place], recv_sem=inc_recv.at[place],
-            device_id=(me, side), device_id_type=MESH,
-        )
-        for place, (origin, target, side) in enumerate(
-            [
-                (inc_out.at[:, :, pl.ds(0, wide)], inc_far.at[:, :, pl.ds(0, wide)], away),
-                (inc_out.at[:, :, pl.ds(wide, wide)], inc_far.at[:, :, pl.ds(wide, wide)], away),
-                (inc_out, inc_pair, pair),
-            ]
-        )
-    ]
-    for copy in passes:
-        copy.start()
-
     half = lax.broadcasted_iota(jnp.int32, (8, 128), 0) < 4
 
-    def lower(source, place, base, blocks):
+    def lower(source, place, base, side, blocks):
+        last = place == 2 and side == 1
+        span_rows = range(side * some, (side + 1) * some)
+        scale = [[theta[row, base + step] for step in range(3)] for row in span_rows]
         for block in blocks:
             lanes = slice(block * 128, (block + 1) * 128)
-            straight = [source[row, :, lanes] for row in range(rows)]
+            straight = [source[row, :, lanes] for row in span_rows]
             crossed = []
-            for row in range(rows):
-                swapped = pltpu.roll(straight[row], 4, 0)
+            for field in straight:
+                swapped = pltpu.roll(field, 4, 0)
                 crossed.append(jnp.where(half, swapped, -swapped))
-            scale = [[theta[row, base + step] for step in range(3)] for row in range(rows)]
             for octant in range(0, 8, 2):
                 sums = [[], [], []]
                 for one in (octant, octant + 1):
                     totals = [jnp.zeros((8, 128), F32)] * 3
-                    for row in range(rows):
+                    for index, row in enumerate(span_rows):
                         piece = (
-                            straight[row] * cosine[place, row, one : one + 1, lanes]
-                            + crossed[row] * sine[place, row, one : one + 1, lanes]
+                            straight[index] * cosine[place, row, one : one + 1, lanes]
+                            + crossed[index] * sine[place, row, one : one + 1, lanes]
                         )
-                        totals = [total + scale[row][step] * piece for step, total in enumerate(totals)]
+                        totals = [total + scale[index][step] * piece for step, total in enumerate(totals)]
                     for step in range(3):
                         sums[step].append(totals[step])
                 for step in range(3):
                     span = slice(step * 64 + octant * 8, step * 64 + octant * 8 + 16)
                     value = jnp.concatenate(sums[step], axis=0)
-                    if place > 0:
+                    if place > 0 or side > 0:
                         value = value + total_low[span, lanes]
-                    if place < 2:
+                    if not last:
                         total_low[span, lanes] = value
                     else:
                         high, low = halves(value)
@@ -351,14 +335,46 @@
                         low_lo[span, lanes] = low
 
     blocks = azimuth // 128
-    lower(inc_out, 0, 3, range(blocks))
-    passes[2].wait()
-    lower(inc_pair, 1, 6 * core, range(blocks))
-    pltpu.make_async_copy(msg_out.at[others], msg_in.at[others], a2a_send).wait()
-    pltpu.make_async_copy(back_out.at[others], back_in.at[others], back_send).wait()
+    wide = azimuth // 2
+
+    def hand(origin, target, place, side):
+        copy = pltpu.make_async_remote_copy(
+            src_ref=origin, dst_ref=target, send_sem=inc_send.at[place], recv_sem=inc_recv.at[place],
+            device_id=(me, side), device_id_type=MESH,
+        )
+        copy.start()
+        return copy
+
+    passes = []
+    for side in range(2):
+        owns[side].wait()
+        pltpu.make_async_copy(back_out.at[side, others], back_in.at[side, others], back_recv.at[side]).wait()
+        for row in range(some):
+            field = swap_groups(back_in[side, :, row, :].reshape(n_clus // 8, 8, 128))
+            for block in range(blocks):
+                inc_out[side * some + row, :, block * 128 : (block + 1) * 128] = field[block]
+        span = pl.ds(side * some, some)
+        if side == 0:
+            passes.append(hand(inc_out.at[span], inc_far.at[span], 0, away))
+            passes.append(hand(inc_out.at[span], inc_pair.at[span], 1, pair))
+        else:
+            for part in range(2):
+                cols = pl.ds(part * wide, wide)
+                passes.append(hand(inc_out.at[span, :, cols], inc_far.at[span, :, cols], 2 + part, away))
+            passes.append(hand(inc_out.at[span], inc_pair.at[span], 4, pair))
+        lower(inc_out, 0, 3, side, range(blocks))
+    passes[1].wait()
+    lower(inc_pair, 1, 6 * core, 0, range(blocks))
+    passes[4].wait()
+    lower(inc_pair, 1, 6 * core, 1, range(blocks))
+    for side in range(2):
+        pltpu.make_async_copy(msg_out.at[side, others], msg_in.at[side, others], a2a_send.at[side]).wait()
+        pltpu.make_async_copy(back_out.at[side, others], back_in.at[side, others], back_send.at[side]).wait()
+    passes[0].wait()
+    lower(inc_far, 2, 6 - 6 * core, 0, range(blocks))
     for part in range(2):
-        passes[part].wait()
-        lower(inc_far, 2, 6 - 6 * core, range(part * blocks // 2, (part + 1) * blocks // 2))
+        passes[2 + part].wait()
+        lower(inc_far, 2, 6 - 6 * core, 1, range(part * blocks // 2, (part + 1) * blocks // 2))
         lanes = slice(part * wide, (part + 1) * wide)
         for cut in range(0, columns, 256):
             span = slice(cut, cut + 256)
@@ -385,7 +401,7 @@
     phase = shift_phase.transpose(1, 0, 2)
     table = translation_table.transpose(0, 2, 1, 3)
     far, vec = far_list.T, far_vector.T
-    mail = pltpu.VMEM((n_clus, rows, 128), F32)
+    mail = pltpu.VMEM((2, n_clus, rows // 2, 128), F32)
     incoming, child_incoming = pl.pallas_call(
         functools.partial(window, n_clus, n_samp),
         out_shape=(jax.ShapeDtypeStruct(field, F32), jax.ShapeDtypeStruct(block, F32)),
@@ -403,7 +419,7 @@
             pltpu.VMEM((3,) + field, F32),
             pltpu.VMEM((3,) + field, F32),
             pltpu.VMEM((4, far_count * 64, clusters), BF16),
-            pltpu.VMEM((4, far_count * 64, 256), F32),
+            pltpu.VMEM((2, 4, far_count * 64, 128), F32),
             pltpu.VMEM(block, F32),
             pltpu.VMEM(block, F32),
             pltpu.VMEM((rows * 64, columns), BF16),
@@ -422,13 +438,13 @@
             pltpu.SemaphoreType.DMA((2,)),
             pltpu.SemaphoreType.DMA((2,)),
             pltpu.SemaphoreType.DMA((2,)),
-            pltpu.SemaphoreType.DMA,
-            pltpu.SemaphoreType.DMA,
-            pltpu.SemaphoreType.DMA((2,)),
-            pltpu.SemaphoreType.DMA,
-            pltpu.SemaphoreType.DMA,
-            pltpu.SemaphoreType.DMA((3,)),
-            pltpu.SemaphoreType.DMA((3,)),
+            pltpu.SemaphoreType.DMA((2,)),
+            pltpu.SemaphoreType.DMA((2,)),
+            pltpu.SemaphoreType.DMA((4,)),
+            pltpu.SemaphoreType.DMA((2,)),
+            pltpu.SemaphoreType.DMA((2,)),
+            pltpu.SemaphoreType.DMA((5,)),
+            pltpu.SemaphoreType.DMA((5,)),
             pltpu.SemaphoreType.REGULAR((2,)),
         ],
         compiler_params=pltpu.CompilerParams(collective_id=0, has_side_effects=True, vmem_limit_bytes=48 << 20),

time: 67.9 us -> 63.5 us (0.935)
  Pallas kernels: 62.9 us -> 58.5 us
    pallas_call x1, Pallas kernels: 62.9 us -> 58.5 us  [per_device(): pl.pallas_call(functools.partial(window, n_clus, n_samp), out_shape=(jax....]
where the time goes in v5:
time: 63.5 us; the launch traced here: 63.4 us
  Pallas kernels  58.5 us (92%)
  local copies, waits for them, and re-layouts  4.14 us (7%)
  between operations  0.73 us (1%)
    pallas_call x1, Pallas kernels, per_device(): pl.pallas_call(functools.partial(window, n_clus, n_samp), out_shape=(jax....  58.5 us

profile of v5, /device:TPU:1, one launch (start us, length us, event | category | flops | bytes accessed | tf_op | source)
XLA Modules:
  0.0 63.4 jit_solution(9086328287988524995)
XLA Ops:
  0.6 1.3 %copy.15 = f32[4,8,2,3,512]{4,0,2,1,3:T(4,128)S(1)} copy(f32[4,8,2,3,512]{4,2,3,1,0:T(2,128)} %bitcast.23) | data formatting | bytes 786432 | tf_op jit(solution)/shard_map/reshape | solution.py:393
  1.9 0.0 copy-start
  1.9 0.0 copy-start.1
  1.9 0.0 copy-start.2
  1.9 0.0 copy-start.3
  1.9 0.0 copy-start.4
  1.9 0.0 copy-start.5
  2.0 0.0 copy-start.6
  2.0 0.1 reshape.20.child
  2.1 0.7 %copy-done = f32[8,6,1024]{2,0,1:T(8,128)S(1)} copy-done((f32[8,6,1024]{2,0,1:T(8,128)S(1)}, f32[8,6,1024]{2,0,1:T(8,128)}, u32[]{:S(2)}) %copy-start) | copy-done | bytes 196632
  2.8 0.1 copy-done.1
  2.9 0.0 copy-done.2
  2.9 0.0 copy-done.3
  2.9 0.0 copy-done.4
  2.9 0.0 copy-done.5
  2.9 0.0 copy-done.6
  2.9 58.5 %shard_map.95 = (f32[6,8,1024]{2,1,0:T(8,128)S(1)}, f32[3,64,512]{2,1,0:T(8,128)S(1)}) custom-call(f32[6,9]{1,0:T(8,128)S(1)} %copy-done.6, f32[3,64,512]{2,1,0:T(8,128)S(1)} %reshape.20.child, s32[6,1024]{1,0:T(8,128)S(1)} %bitcast.17, f32[6,1024]{1,0:T(8,128)S(1)} %bitcast.18, f32[6,8,1024]{2,1,0:T(8,128)S(1)} %bitcast.15, f32[16,6,2,16]{3,2,1,0:T(2,128)S(1)} %bitcast.16, ...), custom_call_target="tpu_custom_call" | custom-call | tf_op jit(solution)/shard_map/pallas_call | solution.py:405
  61.4 0.1 reshape.21
  61.5 0.8 %copy.16 = f32[6,2,4,1024]{3,1,0,2:T(2,128)} copy(f32[6,2,4,1024]{3,2,1,0:T(4,128)S(1)} %reshape.21) | data formatting | bytes 393216 | tf_op jit(solution)/shard_map/reshape | solution.py:452
  62.3 0.1 reshape.22
  62.4 0.9 %copy.12 = f32[4,8,2,3,512]{4,2,3,1,0:T(2,128)} copy(f32[4,8,2,3,512]{4,0,2,1,3:T(4,128)S(1)} %bitcast.21) | data formatting | bytes 786432 | tf_op jit(solution)/shard_map/transpose | solution.py:453
Async XLA Ops:
  1.9 0.9 %copy-start = (f32[8,6,1024]{2,0,1:T(8,128)S(1)}, f32[8,6,1024]{2,0,1:T(8,128)}, u32[]{:S(2)}) copy-start(f32[8,6,1024]{2,0,1:T(8,128)} %param.12) | copy-start | bytes 589828
  1.9 1.0 %copy-start.1 = (f32[16,2,6,16]{3,1,2,0:T(2,128)S(1)}, f32[16,2,6,16]{3,1,2,0:T(2,128)}, u32[]{:S(2)}) copy-start(f32[16,2,6,16]{3,1,2,0:T(2,128)} %param.13) | copy-start | bytes 36868
  1.9 1.0 %copy-start.2 = (s32[1024,6]{0,1:T(8,128)S(1)}, s32[1024,6]{0,1:T(8,128)}, u32[]{:S(2)}) copy-start(s32[1024,6]{0,1:T(8,128)} %param.10) | copy-start | bytes 73732
  1.9 1.0 %copy-start.3 = (f32[1024,6]{0,1:T(8,128)S(1)}, f32[1024,6]{0,1:T(8,128)}, u32[]{:S(2)}) copy-start(f32[1024,6]{0,1:T(8,128)} %param.11) | copy-start | bytes 73732
  1.9 1.0 %copy-start.4 = (s32[256,12]{0,1:T(8,128)S(1)}, s32[256,12]{0,1:T(8,128)}, u32[]{:S(2)}) copy-start(s32[256,12]{0,1:T(8,128)} %param.14) | copy-start | bytes 36868
  1.9 0.9 %copy-start.5 = (s32[256,12]{0,1:T(8,128)S(1)}, s32[256,12]{0,1:T(8,128)}, u32[]{:S(2)}) copy-start(s32[256,12]{0,1:T(8,128)} %param.15) | copy-start | bytes 36868
  2.0 0.9 %copy-start.6 = (f32[6,9]{1,0:T(8,128)S(1)}, f32[6,9]{1,0:T(8,128)}, u32[]{:S(2)}) copy-start(f32[6,9]{1,0:T(8,128)} %theta.1) | copy-start | bytes 652

commit v6 on v5

--- a/solution.py
+++ b/solution.py
@@ -184,25 +184,30 @@
         lhs_lo[row * 64 : (row + 1) * 64, :] = low
 
     pl.semaphore_wait(zone.at[1], 2)
-    seat = lax.rem(me, 16)
     half_w = lax.broadcasted_iota(jnp.int32, (8, 256), 0) < 4
     turns = (2, 1, 3, 0)
 
     def mail_plane(turn, outbox, inbox, send_sem, recv_sem):
         block = lax.rem(plane + turn, 4)
 
-        def send(step, carry):
-            target = block * 16 + lax.rem(seat + step, 16)
+        def send(rise, turned):
+            target = block * 16 + lax.rem(deep + rise, 4) * 4 + lax.rem(across + turned, 4)
             pltpu.make_async_remote_copy(
                 src_ref=outbox.at[target], dst_ref=inbox.at[me], send_sem=send_sem, recv_sem=recv_sem,
                 device_id=(target, ring), device_id_type=MESH,
             ).start()
-            return carry
-
-        if turn == 0:
-            lax.fori_loop(1, 16, send, 0)
-        else:
-            lax.fori_loop(4, 20, send, 0)
+
+        @pl.loop(0, 4)
+        def _(step):
+            send(2, step)
+
+        @pl.loop(0, 8)
+        def _(step):
+            send(1 + 2 * lax.rem(step, 2), lax.div(step, 2))
+
+        @pl.loop(1 if turn == 0 else 0, 4)
+        def _(step):
+            send(0, step)
 
     def spans(turn):
         return pl.ds(pl.multiple_of(lax.rem(plane + turn, 4) * 256, 256), 256)
@@ -255,11 +260,11 @@
             for row in range(some):
                 total = jnp.where(group == row, pltpu.roll(arrived[row], (16 * (row - seat_in)) % 128, 1), total)
             gathered.append(total)
-        x_hi, x_lo = halves(jnp.concatenate(gathered, axis=0))
+        both = jnp.concatenate(halves(jnp.concatenate(gathered, axis=0)), axis=1)
 
         def fetch(turn):
-            pick = picks[lax.rem(plane + turn, 4)]
-            return dot(pick, x_hi, ((1,), (0,))) + dot(pick, x_lo, ((1,), (0,)))
+            found = dot(picks[lax.rem(plane + turn, 4)], both, ((1,), (0,)))
+            return found[:, :128] + found[:, 128:]
 
         source = fetch(turns[0])
         for place, turn in enumerate(turns):
@@ -448,7 +453,7 @@
             pltpu.SemaphoreType.REGULAR((2,)),
         ],
         compiler_params=pltpu.CompilerParams(collective_id=0, has_side_effects=True, vmem_limit_bytes=48 << 20),
-    )(theta_weights, child, stencil, weights, phase, table, far, vec)
+    )(theta_weights, child, *(pltpu.with_memory_space_constraint(x, pltpu.HBM) for x in (stencil, weights, phase, table, far, vec)))
     incoming = incoming.reshape(rows, 2, groups, azimuth).transpose(2, 1, 0, 3)
     child_incoming = child_incoming.reshape(own_rows, 8, 2, groups, columns).transpose(3, 1, 2, 0, 4)
     return incoming, child_incoming.reshape(child_patterns.shape)

time: 63.5 us -> 63.5 us (level)
  no operation moved by 1% of the time
where the time goes in v6:
time: 63.5 us; the launch traced here: 63.3 us
  Pallas kernels  58.8 us (93%)
  local copies, waits for them, and re-layouts  3.87 us (6%)
  between operations  0.67 us (1%)
    pallas_call x1, Pallas kernels, per_device(): pl.pallas_call(functools.partial(window, n_clus, n_samp), out_shape=(jax....  58.8 us

profile of v6, /device:TPU:1, one launch (start us, length us, event | category | flops | bytes accessed | tf_op | source)
XLA Modules:
  0.0 63.3 jit_solution(4430518931674855464)
XLA Ops:
  0.6 1.3 %copy.15 = f32[4,8,2,3,512]{4,0,2,1,3:T(4,128)S(1)} copy(f32[4,8,2,3,512]{4,2,3,1,0:T(2,128)} %bitcast.17) | data formatting | bytes 786432 | tf_op jit(solution)/shard_map/reshape | solution.py:398
  1.9 0.0 copy-start
  1.9 0.1 reshape.20.child
  2.0 0.5 copy-done
  2.6 58.8 %shard_map.95 = (f32[6,8,1024]{2,1,0:T(8,128)S(1)}, f32[3,64,512]{2,1,0:T(8,128)S(1)}) custom-call(f32[6,9]{1,0:T(8,128)S(1)} %copy-done, f32[3,64,512]{2,1,0:T(8,128)S(1)} %reshape.20.child, s32[6,1024]{1,0:T(8,128)} %bitcast.22, f32[6,1024]{1,0:T(8,128)} %bitcast.23, f32[6,8,1024]{2,1,0:T(8,128)} %bitcast.20, f32[16,6,2,16]{3,2,1,0:T(2,128)} %bitcast.21, ...), custom_call_target="tpu_custom_call" | custom-call | tf_op jit(solution)/shard_map/pallas_call | solution.py:410
  61.4 0.1 reshape.21
  61.4 0.8 %copy.16 = f32[6,2,4,1024]{3,1,0,2:T(2,128)} copy(f32[6,2,4,1024]{3,2,1,0:T(4,128)S(1)} %reshape.21) | data formatting | bytes 393216 | tf_op jit(solution)/shard_map/reshape | solution.py:457
  62.2 0.1 reshape.22
  62.4 0.9 %copy.12 = f32[4,8,2,3,512]{4,2,3,1,0:T(2,128)} copy(f32[4,8,2,3,512]{4,0,2,1,3:T(4,128)S(1)} %bitcast.15) | data formatting | bytes 786432 | tf_op jit(solution)/shard_map/transpose | solution.py:458
Async XLA Ops:
  1.9 0.7 %copy-start = (f32[6,9]{1,0:T(8,128)S(1)}, f32[6,9]{1,0:T(8,128)}, u32[]{:S(2)}) copy-start(f32[6,9]{1,0:T(8,128)} %theta.1) | copy-start | bytes 652
